TPU v7x, 32 devices: a whole 2x2x4 slice. The times are simulated.
32 devices in a mesh: dp: 4 (over x, core), expert: 8 (over z, y).
Axes of the slice: x: 2, y: 2, z: 4, core: 2. Of those that a mesh axis runs over, the one named last changes fastest.
Arguments:
- patches: bfloat16 [3, 16384, 384], P(None, ('dp', 'expert')), may hold values from -6 to 6
- out_grad: bfloat16 [3, 16384, 384], P(None, ('dp', 'expert')), may hold values from -6 to 6
- item_ids: int32 [3, 32, 512], P(None, ('dp', 'expert')), may hold values from 0 to 7, never falling along the last dimension, each value on 1 to 128 neighbouring positions
- expert_ids: int32 [3, 16384, 2], P(None, ('dp', 'expert')), may hold values from 0 to 7, all different within a row; in each aligned block of 512 rows (0 to 511, 512 to 1023, ..., all dimensions but the last counted through in order) at most 256 rows name the same one
- qkv_master: float32 [384, 1152], replicated, may hold values from -0.3125 to 0.3125
- qkv_first: float32 [384, 1152], replicated
- qkv_second: float32 [384, 1152], replicated, as said below
- proj_master: float32 [384, 384], replicated, may hold values from -1.25 to 1.25
- proj_first: float32 [384, 384], replicated
- proj_second: float32 [384, 384], replicated, as said below
- router_master: float32 [384, 8], replicated, may hold values from -0.21875 to 0.21875
- router_first: float32 [384, 8], replicated
- router_second: float32 [384, 8], replicated, as said below
- gains_master: float32 [2, 384], replicated, may hold values from 0.5 to 1.5
- gains_first: float32 [2, 384], replicated
- gains_second: float32 [2, 384], replicated, as said below
- inner_master: float32 [8, 384, 1536], P('expert', 'dp'), may hold values from -0.3125 to 0.3125
- inner_first: float32 [8, 384, 1536], P('expert', 'dp')
- inner_second: float32 [8, 384, 1536], P('expert', 'dp'), as said below
- down_master: float32 [8, 768, 384], P('expert', 'dp'), may hold values from -0.4375 to 0.4375
- down_first: float32 [8, 768, 384], P('expert', 'dp')
- down_second: float32 [8, 768, 384], P('expert', 'dp'), as said below
Outputs:
- block_out: bfloat16 [3, 16384, 384], P(None, ('dp', 'expert'))
- patch_grad: float32 [3, 16384, 384], P(None, ('dp', 'expert'))
- qkv_updated: float32 [384, 1152], replicated
- qkv_first_new: float32 [384, 1152], replicated
- qkv_second_new: float32 [384, 1152], replicated
- proj_updated: float32 [384, 384], replicated
- proj_first_new: float32 [384, 384], replicated
- proj_second_new: float32 [384, 384], replicated
- router_updated: float32 [384, 8], replicated
- router_first_new: float32 [384, 8], replicated
- router_second_new: float32 [384, 8], replicated
- gains_updated: float32 [2, 384], replicated
- gains_first_new: float32 [2, 384], replicated
- gains_second_new: float32 [2, 384], replicated
- inner_updated: float32 [8, 384, 1536], P('expert', 'dp')
- inner_first_new: float32 [8, 384, 1536], P('expert', 'dp')
- inner_second_new: float32 [8, 384, 1536], P('expert', 'dp')
- down_updated: float32 [8, 768, 384], P('expert', 'dp')
- down_first_new: float32 [8, 768, 384], P('expert', 'dp')
- down_second_new: float32 [8, 768, 384], P('expert', 'dp')
Inputs may be any that keep to these rules, and one draw needn't show every extreme that they name: `expert_ids`: each row names 2 different experts. In each aligned block of 512 rows of a micro-batch (the rows of one device) no expert is named by more than 256 rows, and some expert reaches 256. `item_ids`: within each pack of 512 tokens the item numbers never fall; an item holds 1 to 128 tokens, and some item holds exactly 128. `qkv_second`: all entries positive. `proj_second`: all entries positive. `router_second`: all entries positive. `gains_second`: all entries positive. `inner_second`: all entries positive. `down_second`: all entries positive.
All inputs are finite; a program needn't handle non-finite values.
Results may differ from a plain program's by a relative error of at most 0.013.
The roundings to bfloat16 on the way count: a program that leaves them out, or rounds other values in their place, can miss the bound.
Values may be sent and summed in bfloat16 or wider, within the bound.
A program may use at most 128 MiB of HBM per device.

v0:
```python
import jax
import jax.numpy as jnp
from jax import lax
from jax.sharding import PartitionSpec as P

HEADS = 6
HEAD = 64


norm_eps = 1e-06
adam_eps = 1e-08
correction = 0.875


def rotary_tables(item_row):
    length = item_row.shape[0]
    places = jnp.arange(length, dtype=jnp.int32)
    starts = jnp.concatenate([jnp.ones((1,), dtype=bool), item_row[1:] != item_row[:-1]])
    first = lax.cummax(jnp.where(starts, places, 0), axis=0)
    offset = (places - first).astype(jnp.float32)
    half = HEAD // 2
    freqs = 10000.0 ** (-jnp.arange(half, dtype=jnp.float32) / half)
    angles = offset[:, None] * freqs[None, :]
    return (jnp.cos(angles), jnp.sin(angles))


def rotate(vectors, cosine, sine):
    half = vectors.shape[-1] // 2
    first_half = vectors[..., :half]
    second_half = vectors[..., half:]
    cos_part = cosine[:, None, :]
    sin_part = sine[:, None, :]
    return jnp.concatenate(
        [
            first_half * cos_part - second_half * sin_part,
            second_half * cos_part + first_half * sin_part,
        ],
        axis=-1,
    )


def masked_scores(query, keys, same_item):
    scores = jnp.einsum("qhe,khe->hqk", query, keys, preferred_element_type=jnp.float32) * 0.125
    return jnp.where(same_item[None], scores, -1e30)


def adamw(weight, first, second, grad, rate, decay):
    first_new = 0.5 * first + 0.5 * grad
    second_new = 0.5 * second + 0.5 * grad * grad
    update = first_new / correction / (jnp.sqrt(second_new / correction) + adam_eps)
    return (weight - rate * (update + decay * weight), first_new, second_new)


def local(
    patches,
    out_grad,
    item_ids,
    expert_ids,
    qkv_master,
    qkv_first,
    qkv_second,
    proj_master,
    proj_first,
    proj_second,
    router_master,
    router_first,
    router_second,
    gains_master,
    gains_first,
    gains_second,
    inner_master,
    inner_first,
    inner_second,
    down_master,
    down_first,
    down_second,
):
    expert_count = lax.axis_size("expert")
    local_experts = inner_master.shape[0]
    experts = expert_count * local_experts
    length = patches.shape[1]
    width = patches.shape[2]
    top = expert_ids.shape[2]
    capacity = 2 * length * top // experts
    hidden_width = down_master.shape[1] * lax.axis_size("dp")
    inner_low, down_low = (
        lax.all_gather(inner_master.astype(jnp.bfloat16), "dp", axis=1, tiled=True),
        lax.all_gather(down_master.astype(jnp.bfloat16), "dp", axis=1, tiled=True),
    )
    qkv_low = qkv_master.astype(jnp.bfloat16)
    proj_low = proj_master.astype(jnp.bfloat16)
    router_low = router_master.astype(jnp.bfloat16)
    gain_attn = gains_master[0]
    gain_ffn = gains_master[1]
    expert_numbers = jnp.arange(experts, dtype=jnp.int32)

    def expert_forward(received):
        count = received.shape[1]
        grid = received.reshape(expert_count, local_experts, count, width)
        both = jnp.einsum("sjcd,jdf->sjcf", grid, inner_low, preferred_element_type=jnp.float32)
        hidden = (jax.nn.silu(both[..., :hidden_width]) * both[..., hidden_width:]).astype(
            jnp.bfloat16
        )
        result = jnp.einsum("sjcf,jfd->sjcd", hidden, down_low, preferred_element_type=jnp.float32)
        result = result.astype(jnp.bfloat16).reshape(experts, count, width)
        returned = lax.all_to_all(result, "expert", split_axis=0, concat_axis=0, tiled=True)
        return (returned, received)

    def micro_step(carry, inputs):
        grad_qkv, grad_proj, grad_router, grad_gains, grad_inner, grad_down = carry
        patch, upstream, item_block, routes = inputs
        items = item_block[0]
        source = patch.astype(jnp.float32)
        inv_first = lax.rsqrt(jnp.mean(source * source, axis=1, keepdims=True) + norm_eps)
        unit_first = source * inv_first
        normed_in = (unit_first * gain_attn).astype(jnp.bfloat16)
        mixed = jnp.dot(normed_in, qkv_low, preferred_element_type=jnp.float32)
        cosine, sine = rotary_tables(items)
        query = rotate(mixed[:, :width].reshape(length, HEADS, HEAD), cosine, sine).astype(
            jnp.bfloat16
        )
        keys = rotate(
            mixed[:, width : 2 * width].reshape(length, HEADS, HEAD), cosine, sine
        ).astype(jnp.bfloat16)
        values = mixed[:, 2 * width :].reshape(length, HEADS, HEAD).astype(jnp.bfloat16)
        same_item = items[:, None] == items[None, :]
        scores = masked_scores(query, keys, same_item)
        peak = jnp.max(scores, axis=2, keepdims=True)
        weights = jnp.exp(scores - peak)
        totals = jnp.sum(weights, axis=2, keepdims=True)
        probs_low = (weights / totals).astype(jnp.bfloat16)
        log_total = peak + jnp.log(totals)
        attended = jnp.einsum("hqk,khe->qhe", probs_low, values, preferred_element_type=jnp.float32)
        attended = attended.reshape(length, width).astype(jnp.bfloat16)
        middle = source + jnp.dot(attended, proj_low, preferred_element_type=jnp.float32)
        inv_second = lax.rsqrt(jnp.mean(middle * middle, axis=1, keepdims=True) + norm_eps)
        unit_second = middle * inv_second
        normed_mid = (unit_second * gain_ffn).astype(jnp.bfloat16)
        logits = jnp.dot(normed_mid, router_low, preferred_element_type=jnp.float32)
        chosen = jnp.take_along_axis(logits, routes, axis=1)
        gates = jax.nn.softmax(chosen, axis=1)
        flat_ids = routes.reshape(length * top)
        hits = (flat_ids[:, None] == expert_numbers[None, :]).astype(jnp.int32)
        rank = jnp.sum(jnp.cumsum(hits, axis=0) * hits, axis=1) - 1
        slots = flat_ids * capacity + rank
        copies = jnp.repeat(normed_mid, top, axis=0)
        outgoing = jnp.zeros((experts * capacity, width), jnp.bfloat16).at[slots].set(copies)
        outgoing = outgoing.reshape(experts, capacity, width)
        returned, kept_inputs = expert_forward(
            lax.all_to_all(outgoing, "expert", split_axis=0, concat_axis=0, tiled=True)
        )
        picked = (
            returned.reshape(experts * capacity, width)[slots]
            .reshape(length, top, width)
            .astype(jnp.float32)
        )
        combined = jnp.sum(gates[:, :, None] * picked, axis=1)
        block_out = (middle + combined).astype(jnp.bfloat16)
        upstream_full = upstream.astype(jnp.float32)
        grad_gate = jnp.sum(upstream_full[:, None, :] * picked, axis=2)
        grad_chosen = gates * (grad_gate - jnp.sum(gates * grad_gate, axis=1, keepdims=True))
        route_hits = (routes[:, :, None] == expert_numbers[None, None, :]).astype(jnp.float32)
        grad_logits = jnp.sum(grad_chosen[:, :, None] * route_hits, axis=1).astype(jnp.bfloat16)
        grad_router_now = jnp.dot(normed_mid.T, grad_logits, preferred_element_type=jnp.float32)
        grad_mid = jnp.dot(grad_logits, router_low.T, preferred_element_type=jnp.float32)
        grad_slots = (
            (gates[:, :, None] * upstream_full[:, None, :])
            .astype(jnp.bfloat16)
            .reshape(length * top, width)
        )
        grad_outgoing = (
            jnp.zeros((experts * capacity, width), jnp.bfloat16).at[slots].set(grad_slots)
        )
        grad_outgoing = grad_outgoing.reshape(experts, capacity, width)
        incoming, inputs_back = (
            lax.all_to_all(grad_outgoing, "expert", split_axis=0, concat_axis=0, tiled=True),
            lax.all_to_all(outgoing, "expert", split_axis=0, concat_axis=0, tiled=True),
        )
        grid_in = inputs_back.reshape(expert_count, local_experts, capacity, width)
        grid_grad = incoming.reshape(expert_count, local_experts, capacity, width)
        both = jnp.einsum("sjcd,jdf->sjcf", grid_in, inner_low, preferred_element_type=jnp.float32)
        gate_part = both[..., :hidden_width]
        up_part = both[..., hidden_width:]
        sigma = jax.nn.sigmoid(gate_part)
        activated = jax.nn.silu(gate_part)
        hidden = (activated * up_part).astype(jnp.bfloat16)
        grad_hidden = jnp.einsum(
            "sjcd,jfd->sjcf", grid_grad, down_low, preferred_element_type=jnp.float32
        )
        grad_down_now = jnp.einsum(
            "sjcf,sjcd->jfd", hidden, grid_grad, preferred_element_type=jnp.float32
        )
        grad_both = jnp.concatenate(
            [
                grad_hidden * up_part * sigma * (1.0 + gate_part * (1.0 - sigma)),
                grad_hidden * activated,
            ],
            axis=3,
        ).astype(jnp.bfloat16)
        grad_inner_now = jnp.einsum(
            "sjcd,sjcf->jdf", grid_in, grad_both, preferred_element_type=jnp.float32
        )
        grad_copies = jnp.einsum(
            "sjcf,jdf->sjcd", grad_both, inner_low, preferred_element_type=jnp.float32
        )
        grad_copies = grad_copies.astype(jnp.bfloat16).reshape(experts, capacity, width)
        grad_back = lax.all_to_all(grad_copies, "expert", split_axis=0, concat_axis=0, tiled=True)
        grad_picked = grad_back.reshape(experts * capacity, width)[slots].reshape(
            length, top, width
        )
        grad_mid = grad_mid + jnp.sum(grad_picked.astype(jnp.float32), axis=1)
        grad_unit_second = grad_mid * gain_ffn
        grad_gain_ffn = jnp.sum(grad_mid * unit_second, axis=0)
        grad_middle = upstream_full + inv_second * (
            grad_unit_second
            - unit_second * jnp.mean(grad_unit_second * unit_second, axis=1, keepdims=True)
        )
        grad_branch = grad_middle.astype(jnp.bfloat16)
        grad_proj_now = jnp.dot(attended.T, grad_branch, preferred_element_type=jnp.float32)
        grad_attended = jnp.dot(grad_branch, proj_low.T, preferred_element_type=jnp.float32)
        grad_attended = grad_attended.astype(jnp.bfloat16).reshape(length, HEADS, HEAD)
        probs_again = jnp.exp(masked_scores(query, keys, same_item) - log_total)
        grad_probs = jnp.einsum(
            "qhe,khe->hqk", grad_attended, values, preferred_element_type=jnp.float32
        )
        grad_values = jnp.einsum(
            "hqk,qhe->khe", probs_low, grad_attended, preferred_element_type=jnp.float32
        )
        grad_scores = probs_again * (
            grad_probs - jnp.sum(probs_again * grad_probs, axis=2, keepdims=True)
        )
        grad_scores = grad_scores.astype(jnp.bfloat16)
        grad_query = (
            jnp.einsum("hqk,khe->qhe", grad_scores, keys, preferred_element_type=jnp.float32)
            * 0.125
        )
        grad_keys = (
            jnp.einsum("hqk,qhe->khe", grad_scores, query, preferred_element_type=jnp.float32)
            * 0.125
        )
        grad_mixed = jnp.concatenate(
            [
                rotate(grad_query, cosine, -sine).reshape(length, width),
                rotate(grad_keys, cosine, -sine).reshape(length, width),
                grad_values.reshape(length, width),
            ],
            axis=1,
        ).astype(jnp.bfloat16)
        grad_qkv_now = jnp.dot(normed_in.T, grad_mixed, preferred_element_type=jnp.float32)
        grad_normed = jnp.dot(grad_mixed, qkv_low.T, preferred_element_type=jnp.float32)
        grad_unit_first = grad_normed * gain_attn
        grad_gain_attn = jnp.sum(grad_normed * unit_first, axis=0)
        patch_grad = grad_middle + inv_first * (
            grad_unit_first
            - unit_first * jnp.mean(grad_unit_first * unit_first, axis=1, keepdims=True)
        )
        new_carry = (
            grad_qkv + grad_qkv_now,
            grad_proj + grad_proj_now,
            grad_router + grad_router_now,
            grad_gains + jnp.stack([grad_gain_attn, grad_gain_ffn]),
            grad_inner + grad_inner_now,
            grad_down + grad_down_now,
        )
        return (new_carry, (block_out, patch_grad))

    start = (
        jnp.zeros(qkv_master.shape, jnp.float32),
        jnp.zeros(proj_master.shape, jnp.float32),
        jnp.zeros(router_master.shape, jnp.float32),
        jnp.zeros(gains_master.shape, jnp.float32),
        jnp.zeros(inner_low.shape, jnp.float32),
        jnp.zeros(down_low.shape, jnp.float32),
    )
    totals, outputs = lax.scan(micro_step, start, (patches, out_grad, item_ids, expert_ids))
    grad_qkv, grad_proj, grad_router, grad_gains = lax.psum(
        (totals[0], totals[1], totals[2], totals[3]), ("dp", "expert")
    )
    grad_inner, grad_down = (
        lax.psum_scatter(totals[4], "dp", scatter_dimension=1, tiled=True),
        lax.psum_scatter(totals[5], "dp", scatter_dimension=1, tiled=True),
    )
    qkv_new = adamw(qkv_master, qkv_first, qkv_second, grad_qkv, 0.1, 0.1)
    proj_new = adamw(proj_master, proj_first, proj_second, grad_proj, 0.4, 0.1)
    router_new = adamw(router_master, router_first, router_second, grad_router, 0.07, 0.1)
    gains_new = adamw(gains_master, gains_first, gains_second, grad_gains, 0.4, 0.0)
    inner_new = adamw(inner_master, inner_first, inner_second, grad_inner, 0.1, 0.1)
    down_new = adamw(down_master, down_first, down_second, grad_down, 0.15, 0.1)
    return (
        outputs[0],
        outputs[1],
        qkv_new[0],
        qkv_new[1],
        qkv_new[2],
        proj_new[0],
        proj_new[1],
        proj_new[2],
        router_new[0],
        router_new[1],
        router_new[2],
        gains_new[0],
        gains_new[1],
        gains_new[2],
        inner_new[0],
        inner_new[1],
        inner_new[2],
        down_new[0],
        down_new[1],
        down_new[2],
    )


def solution(mesh):
    in_specs = (
        P(None, ("dp", "expert"), None),
        P(None, ("dp", "expert"), None),
        P(None, ("dp", "expert"), None),
        P(None, ("dp", "expert"), None),
        P(),
        P(),
        P(),
        P(),
        P(),
        P(),
        P(),
        P(),
        P(),
        P(),
        P(),
        P(),
        P("expert", "dp", None),
        P("expert", "dp", None),
        P("expert", "dp", None),
        P("expert", "dp", None),
        P("expert", "dp", None),
        P("expert", "dp", None),
    )
    out_specs = (
        P(None, ("dp", "expert"), None),
        P(None, ("dp", "expert"), None),
        P(),
        P(),
        P(),
        P(),
        P(),
        P(),
        P(),
        P(),
        P(),
        P(),
        P(),
        P(),
        P("expert", "dp", None),
        P("expert", "dp", None),
        P("expert", "dp", None),
        P("expert", "dp", None),
        P("expert", "dp", None),
        P("expert", "dp", None),
    )
    return jax.shard_map(local, mesh=mesh, in_specs=in_specs, out_specs=out_specs, check_vma=False)
```

profile of v0, /device:TPU:0, one launch (start us, length us, event | category | flops | bytes accessed | tf_op | source)
XLA Modules:
  0.0 987.1 jit_solution(13137840849354366140)
XLA Ops:
  14.3 9.5 all_gather.7
  30.3 750.3 %while.28 = (s32[]{:T(128)}, f32[384,1152]{1,0:T(8,128)}, f32[384,384]{1,0:T(8,128)}, f32[384,8]{0,1:T(8,128)}, f32[2,384]{1,0:T(2,128)}, /*index=5*/f32[1,384,1...) while((s32[]{:T(128)}, f32[384,1152]{1,0:T(8,128)}, ...), condition=%wide.region_24.25_spmd.clone.clone, body=%wide.region_0.24_spmd.clone.clone.sunk | while | flops 14020268032 | bytes 440514304 | solution.py:275
  87.5 18.1 %all-to-all-done = bf16[8,256,384]{2,1,0:T(8,128)(2,1)} async-done(((bf16[8,256,384]{2,1,0:T(8,128)(2,1)}), bf16[8,256,384]{2,1,0:T(8,128)(2,1)}, u32[]{:S(2)}, u32[]{:S(2)}) %all-to-all-start) | async-done | bytes 1572896 | tf_op jit(solution)/shard_map/while/body/eval_jaxpr/all_to_all | solution.py:150
  109.9 9.7 convolution_bitcast_fusion.3
  119.7 27.4 %all-to-all-done.1 = bf16[8,256,384]{2,1,0:T(8,128)(2,1)S(1)} async-done(((bf16[8,256,384]{2,1,0:T(8,128)(2,1)}), bf16[8,256,384]{2,1,0:T(8,128)(2,1)S(1)}, u32[]{:S(2)}, u32[]{:S(2)}) %all-to-all-start.1) | async-done | bytes 1572896 | tf_op jit(solution)/shard_map/while/body/eval_jaxpr/all_to_all | solution.py:176
  147.0 8.7 fusion.221
  164.2 7.5 fusion.223
  171.7 29.6 %all-to-all-done.2 = bf16[8,256,384]{2,1,0:T(8,128)(2,1)S(1)} async-done(((bf16[8,256,384]{2,1,0:T(8,128)(2,1)}), bf16[8,256,384]{2,1,0:T(8,128)(2,1)S(1)}, u32[]{:S(2)}, u32[]{:S(2)}) %all-to-all-start.2) | async-done | bytes 1572896 | tf_op jit(solution)/shard_map/while/body/eval_jaxpr/all_to_all | solution.py:106
  335.4 17.3 %all-to-all-done = bf16[8,256,384]{2,1,0:T(8,128)(2,1)} async-done(((bf16[8,256,384]{2,1,0:T(8,128)(2,1)}), bf16[8,256,384]{2,1,0:T(8,128)(2,1)}, u32[]{:S(2)}, u32[]{:S(2)}) %all-to-all-start) | async-done | bytes 1572896 | tf_op jit(solution)/shard_map/while/body/eval_jaxpr/all_to_all | solution.py:150
  356.6 9.7 convolution_bitcast_fusion.3
  366.3 27.4 %all-to-all-done.1 = bf16[8,256,384]{2,1,0:T(8,128)(2,1)S(1)} async-done(((bf16[8,256,384]{2,1,0:T(8,128)(2,1)}), bf16[8,256,384]{2,1,0:T(8,128)(2,1)S(1)}, u32[]{:S(2)}, u32[]{:S(2)}) %all-to-all-start.1) | async-done | bytes 1572896 | tf_op jit(solution)/shard_map/while/body/eval_jaxpr/all_to_all | solution.py:176
  393.7 8.7 fusion.221
  410.9 7.5 fusion.223
  418.3 29.6 %all-to-all-done.2 = bf16[8,256,384]{2,1,0:T(8,128)(2,1)S(1)} async-done(((bf16[8,256,384]{2,1,0:T(8,128)(2,1)}), bf16[8,256,384]{2,1,0:T(8,128)(2,1)S(1)}, u32[]{:S(2)}, u32[]{:S(2)}) %all-to-all-start.2) | async-done | bytes 1572896 | tf_op jit(solution)/shard_map/while/body/eval_jaxpr/all_to_all | solution.py:106
  583.9 17.3 %all-to-all-done = bf16[8,256,384]{2,1,0:T(8,128)(2,1)} async-done(((bf16[8,256,384]{2,1,0:T(8,128)(2,1)}), bf16[8,256,384]{2,1,0:T(8,128)(2,1)}, u32[]{:S(2)}, u32[]{:S(2)}) %all-to-all-start) | async-done | bytes 1572896 | tf_op jit(solution)/shard_map/while/body/eval_jaxpr/all_to_all | solution.py:150
  605.3 9.7 convolution_bitcast_fusion.3
  615.0 27.4 %all-to-all-done.1 = bf16[8,256,384]{2,1,0:T(8,128)(2,1)S(1)} async-done(((bf16[8,256,384]{2,1,0:T(8,128)(2,1)}), bf16[8,256,384]{2,1,0:T(8,128)(2,1)S(1)}, u32[]{:S(2)}, u32[]{:S(2)}) %all-to-all-start.1) | async-done | bytes 1572896 | tf_op jit(solution)/shard_map/while/body/eval_jaxpr/all_to_all | solution.py:176
  642.4 8.7 fusion.221
  659.6 7.5 fusion.223
  667.0 29.6 %all-to-all-done.2 = bf16[8,256,384]{2,1,0:T(8,128)(2,1)S(1)} async-done(((bf16[8,256,384]{2,1,0:T(8,128)(2,1)}), bf16[8,256,384]{2,1,0:T(8,128)(2,1)S(1)}, u32[]{:S(2)}, u32[]{:S(2)}) %all-to-all-start.2) | async-done | bytes 1572896 | tf_op jit(solution)/shard_map/while/body/eval_jaxpr/all_to_all | solution.py:106
  782.1 38.1 %all-reduce = (f32[384,8]{0,1:T(8,128)}, f32[2,384]{1,0:T(2,128)}) all-reduce(f32[384,8]{0,1:T(8,128)S(1)} %copy-done.63, f32[2,384]{1,0:T(2,128)S(1)} %copy-done.74), channel_id=1, replica_groups=mesh['dp'=4,'expert'=8] {'dp','expert'}, use_global_device_ids=true, to_apply=%region_27.28 | all-reduce | flops 3840 | bytes 30720 | tf_op jit(solution)/shard_map/psum | solution.py:276
  822.9 92.6 %all-reduce.4.cloned.1.call-done = (f32[384,1152]{1,0:T(8,128)}, f32[384,384]{1,0:T(8,128)}) async-done(((f32[384,1152]{1,0:T(8,128)}, f32[384,384]{1,0:T(8,128)}), (f32[384,1152]{1,0:T(8,128)}, f32[384,384]{1,0:T(8,128)})) %all-reduce.4.cloned.1.call-update) | async-done | bytes 2359312 | tf_op jit(solution)/shard_map/psum | solution.py:276
  923.6 19.0 %reduce-scatter.5.cloned.1.call-done = f32[1,192,384]{2,1,0:T(8,128)} async-done(((f32[1,768,384]{2,1,0:T(8,128)}), f32[1,192,384]{2,1,0:T(8,128)}) %reduce-scatter.5.cloned.1.call-update) | async-done | bytes 294928 | tf_op jit(solution)/shard_map/reduce_scatter | solution.py:281
  944.6 33.2 %reduce-scatter.3.cloned.1.call-done = f32[1,96,1536]{2,1,0:T(8,128)} async-done(((f32[1,384,1536]{2,1,0:T(8,128)}), f32[1,96,1536]{2,1,0:T(8,128)}) %reduce-scatter.3.cloned.1.call-update) | async-done | bytes 589840 | tf_op jit(solution)/shard_map/reduce_scatter | solution.py:280
  (836 shorter events, 471.5 us)
Async XLA Ops:
  7.2 23.1 %all-gather.2.cloned.1.call-start = ((), (), s32[]{:S(2)}) async-start(), calls=%async_computation.6 | async-start | bytes 1474560 | tf_op jit(solution)/shard_map/all_gather | solution.py:87
  9.1 906.4 %all-reduce.4.cloned.1.call-start = ((), (), s32[]{:S(2)}) async-start(), calls=%async_computation.9 | async-start | bytes 4718592 | tf_op jit(solution)/shard_map/psum | solution.py:276
  61.9 43.7 %all-to-all-start = ((bf16[8,256,384]{2,1,0:T(8,128)(2,1)}), bf16[8,256,384]{2,1,0:T(8,128)(2,1)}, u32[]{:S(2)}, u32[]{:S(2)}) async-start(bf16[8,256,384]{2,1,0:T(8,128)(2,1)} %bitcast.291), calls=%async_computation | async-start | bytes 3145728 | tf_op jit(solution)/shard_map/while/body/eval_jaxpr/all_to_all | solution.py:150
  105.6 41.4 %all-to-all-start.1 = ((bf16[8,256,384]{2,1,0:T(8,128)(2,1)}), bf16[8,256,384]{2,1,0:T(8,128)(2,1)S(1)}, u32[]{:S(2)}, u32[]{:S(2)}) async-start(bf16[8,256,384]{2,1,0:T(8,128)(2,1)} %bitcast.292), calls=%async_computation.1 | async-start | bytes 3145728 | tf_op jit(solution)/shard_map/while/body/eval_jaxpr/all_to_all | solution.py:176
  160.3 41.0 %all-to-all-start.2 = ((bf16[8,256,384]{2,1,0:T(8,128)(2,1)}), bf16[8,256,384]{2,1,0:T(8,128)(2,1)S(1)}, u32[]{:S(2)}, u32[]{:S(2)}) async-start(bf16[8,256,384]{2,1,0:T(8,128)(2,1)} %convolution_convert_fusion.9), calls=%async_computation.2 | async-start | bytes 3145728 | tf_op jit(solution)/shard_map/while/body/eval_jaxpr/all_to_all | solution.py:106
  201.3 41.0 %all-to-all-start.3 = ((bf16[8,256,384]{2,1,0:T(8,128)(2,1)}), bf16[8,256,384]{2,1,0:T(8,128)(2,1)S(1)}, u32[]{:S(2)}, u32[]{:S(2)}) async-start(bf16[8,256,384]{2,1,0:T(8,128)(2,1)} %fusion.223), calls=%async_computation.3 | async-start | bytes 3145728 | tf_op jit(solution)/shard_map/while/body/eval_jaxpr/all_to_all | solution.py:207
  311.4 41.2 %all-to-all-start = ((bf16[8,256,384]{2,1,0:T(8,128)(2,1)}), bf16[8,256,384]{2,1,0:T(8,128)(2,1)}, u32[]{:S(2)}, u32[]{:S(2)}) async-start(bf16[8,256,384]{2,1,0:T(8,128)(2,1)} %bitcast.291), calls=%async_computation | async-start | bytes 3145728 | tf_op jit(solution)/shard_map/while/body/eval_jaxpr/all_to_all | solution.py:150
  352.7 41.0 %all-to-all-start.1 = ((bf16[8,256,384]{2,1,0:T(8,128)(2,1)}), bf16[8,256,384]{2,1,0:T(8,128)(2,1)S(1)}, u32[]{:S(2)}, u32[]{:S(2)}) async-start(bf16[8,256,384]{2,1,0:T(8,128)(2,1)} %bitcast.292), calls=%async_computation.1 | async-start | bytes 3145728 | tf_op jit(solution)/shard_map/while/body/eval_jaxpr/all_to_all | solution.py:176
  356.6 37.1 %copy-start.52 = (bf16[1,768,384]{2,1,0:T(8,128)(2,1)S(1)}, bf16[1,768,384]{2,1,0:T(8,128)(2,1)}, u32[]{:S(2)}) copy-start(bf16[1,768,384]{2,1,0:T(8,128)(2,1)} %get-tuple-element.936) | copy-start | bytes 1769476 | tf_op jit(solution)/shard_map/while
  407.0 41.0 %all-to-all-start.2 = ((bf16[8,256,384]{2,1,0:T(8,128)(2,1)}), bf16[8,256,384]{2,1,0:T(8,128)(2,1)S(1)}, u32[]{:S(2)}, u32[]{:S(2)}) async-start(bf16[8,256,384]{2,1,0:T(8,128)(2,1)} %convolution_convert_fusion.9), calls=%async_computation.2 | async-start | bytes 3145728 | tf_op jit(solution)/shard_map/while/body/eval_jaxpr/all_to_all | solution.py:106
  448.0 41.1 %all-to-all-start.3 = ((bf16[8,256,384]{2,1,0:T(8,128)(2,1)}), bf16[8,256,384]{2,1,0:T(8,128)(2,1)S(1)}, u32[]{:S(2)}, u32[]{:S(2)}) async-start(bf16[8,256,384]{2,1,0:T(8,128)(2,1)} %fusion.223), calls=%async_computation.3 | async-start | bytes 3145728 | tf_op jit(solution)/shard_map/while/body/eval_jaxpr/all_to_all | solution.py:207
  559.9 41.3 %all-to-all-start = ((bf16[8,256,384]{2,1,0:T(8,128)(2,1)}), bf16[8,256,384]{2,1,0:T(8,128)(2,1)}, u32[]{:S(2)}, u32[]{:S(2)}) async-start(bf16[8,256,384]{2,1,0:T(8,128)(2,1)} %bitcast.291), calls=%async_computation | async-start | bytes 3145728 | tf_op jit(solution)/shard_map/while/body/eval_jaxpr/all_to_all | solution.py:150
  601.2 41.2 %all-to-all-start.1 = ((bf16[8,256,384]{2,1,0:T(8,128)(2,1)}), bf16[8,256,384]{2,1,0:T(8,128)(2,1)S(1)}, u32[]{:S(2)}, u32[]{:S(2)}) async-start(bf16[8,256,384]{2,1,0:T(8,128)(2,1)} %bitcast.292), calls=%async_computation.1 | async-start | bytes 3145728 | tf_op jit(solution)/shard_map/while/body/eval_jaxpr/all_to_all | solution.py:176
  655.7 41.0 %all-to-all-start.2 = ((bf16[8,256,384]{2,1,0:T(8,128)(2,1)}), bf16[8,256,384]{2,1,0:T(8,128)(2,1)S(1)}, u32[]{:S(2)}, u32[]{:S(2)}) async-start(bf16[8,256,384]{2,1,0:T(8,128)(2,1)} %convolution_convert_fusion.9), calls=%async_computation.2 | async-start | bytes 3145728 | tf_op jit(solution)/shard_map/while/body/eval_jaxpr/all_to_all | solution.py:106
  696.6 41.0 %all-to-all-start.3 = ((bf16[8,256,384]{2,1,0:T(8,128)(2,1)}), bf16[8,256,384]{2,1,0:T(8,128)(2,1)S(1)}, u32[]{:S(2)}, u32[]{:S(2)}) async-start(bf16[8,256,384]{2,1,0:T(8,128)(2,1)} %fusion.223), calls=%async_computation.3 | async-start | bytes 3145728 | tf_op jit(solution)/shard_map/while/body/eval_jaxpr/all_to_all | solution.py:207
  780.7 134.8 %copy-start.48 = (f32[384,384]{1,0:T(8,128)S(1)}, f32[384,384]{1,0:T(8,128)}, u32[]{:S(2)}) copy-start(f32[384,384]{1,0:T(8,128)} %param.31) | copy-start | bytes 1769476
  780.7 134.8 %copy-start.53 = (f32[384,384]{1,0:T(8,128)S(1)}, f32[384,384]{1,0:T(8,128)}, u32[]{:S(2)}) copy-start(f32[384,384]{1,0:T(8,128)} %param.32) | copy-start | bytes 1769476
  780.7 134.8 %copy-start.54 = (f32[384,384]{1,0:T(8,128)S(1)}, f32[384,384]{1,0:T(8,128)}, u32[]{:S(2)}) copy-start(f32[384,384]{1,0:T(8,128)} %param.33) | copy-start | bytes 1769476
  780.7 161.9 %reduce-scatter.5.cloned.1.call-start = ((), (), s32[]{:S(2)}) async-start(), calls=%async_computation.8 | async-start | bytes 1474560 | tf_op jit(solution)/shard_map/reduce_scatter | solution.py:281
  781.5 196.4 %reduce-scatter.3.cloned.1.call-start = ((), (), s32[]{:S(2)}) async-start(), calls=%async_computation.7 | async-start | bytes 2949120 | tf_op jit(solution)/shard_map/reduce_scatter | solution.py:280
  782.0 136.2 %copy-start.46 = (f32[384,1152]{1,0:T(8,128)S(1)}, f32[384,1152]{1,0:T(8,128)}, u32[]{:S(2)}) copy-start(f32[384,1152]{1,0:T(8,128)} %param.28) | copy-start | bytes 5308420
  923.6 54.2 %copy-start.49 = (f32[1,96,1536]{2,1,0:T(8,128)S(1)}, f32[1,96,1536]{2,1,0:T(8,128)}, u32[]{:S(2)}) copy-start(f32[1,96,1536]{2,1,0:T(8,128)} %param.40) | copy-start | bytes 1769476
  923.6 54.2 %copy-start.55 = (f32[1,96,1536]{2,1,0:T(8,128)S(1)}, f32[1,96,1536]{2,1,0:T(8,128)}, u32[]{:S(2)}) copy-start(f32[1,96,1536]{2,1,0:T(8,128)} %param.41) | copy-start | bytes 1769476
  923.6 54.2 %copy-start.56 = (f32[1,96,1536]{2,1,0:T(8,128)S(1)}, f32[1,96,1536]{2,1,0:T(8,128)}, u32[]{:S(2)}) copy-start(f32[1,96,1536]{2,1,0:T(8,128)} %param.42) | copy-start | bytes 1769476
  (220 other events, 863.7 us)
Sparse Core Ops, SparseCore 0:
  10.1 20.1 all-gather.1
  780.8 134.6 all-reduce.3
  918.1 24.4 reduce-scatter.4
  945.0 32.8 reduce-scatter.2
where the time goes:
time: 991 us; the launch traced here: 987 us
  waiting for transfers between devices  396 us (40%)
  matrix products  177 us (18%)
  local copies, waits for them, and re-layouts  167 us (17%)
  other arithmetic  127 us (13%)
  starting transfers between devices  50.8 us (5%)
  blocking collectives  47.5 us (5%)
  between operations  14.2 us (1%)
    psum x1, waiting for transfers between devices, local(): lax.psum((totals[0], totals[1], totals[2], totals[3]), ('dp', 'expert'))  92.6 us
    all_to_all x3, waiting for transfers between devices, expert_forward(): lax.all_to_all(result, 'expert', split_axis=0, concat_axis=0, tiled=True)  88.8 us
    all_to_all x3, waiting for transfers between devices, micro_step(): lax.all_to_all(grad_outgoing, 'expert', split_axis=0, concat_axis=0, tile...  82.1 us
    all_to_all x3, waiting for transfers between devices, micro_step(): lax.all_to_all(outgoing, 'expert', split_axis=0, concat_axis=0, tiled=True)  52.7 us
    psum x1, blocking collectives, local(): lax.psum((totals[0], totals[1], totals[2], totals[3]), ('dp', 'expert'))  38.1 us
    reduce_scatter x1, waiting for transfers between devices, local(): lax.psum_scatter(totals[4], 'dp', scatter_dimension=1, tiled=True)  33.2 us
    dot_general x3, matrix products, expert_forward(): jnp.einsum('sjcd,jdf->sjcf', grid, inner_low, preferred_element_type=jnp....  29.2 us
    while x426, local copies, waits for them, and re-layouts  26.3 us
  transfers between devices with their start and end apart: 16, of which 16 were waited for; matrix products, arithmetic and copies ran while one was open for 22% of the time, Pallas kernels for 0%

commit v1 on v0

--- a/solution.py
+++ b/solution.py
@@ -1,6 +1,9 @@
 import jax
 import jax.numpy as jnp
+import numpy as np
 from jax import lax
+from jax.experimental import pallas as pl
+from jax.experimental.pallas import tpu as pltpu
 from jax.sharding import PartitionSpec as P
 
 HEADS = 6
@@ -310,6 +313,455 @@
     )
 
 
+F32 = jnp.float32
+BF16 = jnp.bfloat16
+QB = 128
+
+
+def iota(shape, axis):
+    return lax.broadcasted_iota(jnp.int32, shape, axis)
+
+
+def dot_nn(a, b):
+    return jnp.dot(a, b, preferred_element_type=F32)
+
+
+def dot_nt(a, b):
+    return lax.dot_general(a, b, (((1,), (1,)), ((), ())), preferred_element_type=F32)
+
+
+def dot_tn(a, b):
+    return lax.dot_general(a, b, (((0,), (0,)), ((), ())), preferred_element_type=F32)
+
+
+def swap_halves(v, low_lane):
+    width = v.shape[1]
+    half = HEAD // 2
+    return jnp.where(low_lane, pltpu.roll(v, width - half, 1), pltpu.roll(v, half, 1))
+
+
+def turn(v, cos_row, sin_row, low_lane):
+    return v * cos_row + swap_halves(v, low_lane) * sin_row
+
+
+def rope_table(item_max):
+    half = HEAD // 2
+    offset = np.arange(item_max, dtype=np.float32)
+    freqs = np.float32(10000.0) ** (-np.arange(half, dtype=np.float32) / np.float32(half))
+    angles = (offset[:, None] * freqs[None, :]).astype(np.float32)
+    cosine, sine = np.cos(angles), np.sin(angles)
+    return np.concatenate([cosine] * 4 + [-sine, sine] * 2, axis=1).astype(np.float32)
+
+
+def windows(length):
+    found = []
+    for start in range(0, length, QB):
+        low = max(0, start - QB)
+        high = min(length, start + 2 * QB)
+        found.append((start, low, high))
+    return found
+
+
+def row_norm(values):
+    return lax.rsqrt(jnp.mean(values * values, axis=1, keepdims=True) + norm_eps)
+
+
+def positions(item_row, length):
+    eye = iota((length, length), 0) == iota((length, length), 1)
+    col = jnp.sum(jnp.where(eye, item_row, 0.0), axis=1, keepdims=True)
+    before = jnp.sum(jnp.where(item_row < col, 1.0, 0.0), axis=1, keepdims=True)
+    offset = iota((length, 1), 0) - before.astype(jnp.int32)
+    return col, offset
+
+
+def rope_rows(offset, table, length, width):
+    spots = table.shape[0]
+    pick = jnp.where(iota((length, spots), 1) == offset, 1.0, 0.0)
+    both = jnp.dot(pick, table, precision=lax.Precision.HIGHEST, preferred_element_type=F32)
+    copies = width // 128
+    return (
+        jnp.concatenate([both[:, :128]] * copies, axis=1),
+        jnp.concatenate([both[:, 128:]] * copies, axis=1),
+    )
+
+
+def attend_kernel(patches, items, qkv_w, proj_w, gains, table, mixed_o, probs_o, att_o, mid_o, nm_o):
+    packs, length, width = patches.shape
+    pairs = width // 128
+    low_lane = iota((1, width), 1) % HEAD < HEAD // 2
+    first_head = iota((1, 128), 1) < HEAD
+    mask_a = jnp.where(first_head, 1.0, 0.0).astype(BF16)
+    mask_b = jnp.where(first_head, 0.0, 1.0).astype(BF16)
+    top_rows = iota((128, 1), 0) < HEAD
+
+    def pack(p, carry):
+        source = patches[p].astype(F32)
+        normed = (source * row_norm(source) * gains[0:1, :]).astype(BF16)
+        mixed = dot_nn(normed, qkv_w[...])
+        item_row = items[p].astype(F32)
+        item_col, offset = positions(item_row, length)
+        cos_row, sin_row = rope_rows(offset, table[...], length, width)
+        mixed_o[p, :, :width] = turn(mixed[:, :width], cos_row, sin_row, low_lane).astype(BF16)
+        mixed_o[p, :, width : 2 * width] = turn(
+            mixed[:, width : 2 * width], cos_row, sin_row, low_lane
+        ).astype(BF16)
+        mixed_o[p, :, 2 * width :] = mixed[:, 2 * width :].astype(BF16)
+        for pair in range(pairs):
+            lanes = slice(128 * pair, 128 * pair + 128)
+            key_lanes = slice(width + 128 * pair, width + 128 * pair + 128)
+            values_t = mixed[:, 2 * width + 128 * pair : 2 * width + 128 * pair + 128].T.astype(BF16)
+            for block, (start, low, high) in enumerate(windows(length)):
+                query = mixed_o[p, start : start + QB, lanes] * 0.125
+                query = jnp.concatenate([query * mask_a, query * mask_b], axis=0)
+                scores = dot_nt(mixed_o[p, low:high, key_lanes], query)
+                here = item_row[:, start : start + QB]
+                same = item_col[low:high] == jnp.concatenate([here, here], axis=1)
+                scores = jnp.where(same, scores, -1e30)
+                peak = jnp.max(scores, axis=0, keepdims=True)
+                weights = jnp.exp(scores - peak)
+                total = jnp.sum(weights, axis=0, keepdims=True)
+                probs = (weights * (1.0 / total)).astype(BF16)
+                probs_o[p, pair, block, : high - low] = probs
+                out = dot_nn(values_t[:, low:high], probs)
+                out = jnp.where(top_rows, out[:, :QB], out[:, QB:])
+                att_o[p, start : start + QB, lanes] = out.T.astype(BF16)
+        middle = source + dot_nn(att_o[p], proj_w[...])
+        mid_o[p] = middle
+        nm_o[p] = (middle * row_norm(middle) * gains[1:2, :]).astype(BF16)
+        return carry
+
+    lax.fori_loop(0, packs, pack, 0)
+
+
+def expert_kernel(
+    nm, upstream, ids, router_w, inner_w, down_w,
+    inner_g, down_g, back_o, glog_o,
+    both_s, rank_s, gate_s, gg_s, x_s, hid_s, go_s, gb_s, y_s,
+):
+    packs, length, width = nm.shape
+    experts = router_w.shape[0]
+    hidden_width = down_w.shape[1]
+    cap = x_s.shape[0] // packs
+    expert = pl.program_id(0)
+
+    @pl.when(expert == 0)
+    def _():
+        earlier = jnp.where(iota((length, length), 0) < iota((length, length), 1), 1.0, 0.0).astype(BF16)
+
+        def prepare(p, carry):
+            both_s[p, :, :width] = nm[p]
+            both_s[p, :, width:] = upstream[p]
+            logits = dot_nt(router_w[...], nm[p])
+            number = iota((experts, length), 0)
+            hit0 = number == ids[p, 0:1, :]
+            hit1 = number == ids[p, 1:2, :]
+            chosen0 = jnp.sum(jnp.where(hit0, logits, 0.0), axis=0, keepdims=True)
+            chosen1 = jnp.sum(jnp.where(hit1, logits, 0.0), axis=0, keepdims=True)
+            peak = jnp.maximum(chosen0, chosen1)
+            e0 = jnp.exp(chosen0 - peak)
+            e1 = jnp.exp(chosen1 - peak)
+            total = e0 + e1
+            gate_s[p] = jnp.where(hit0, e0 / total, 0.0) + jnp.where(hit1, e1 / total, 0.0)
+            named = jnp.where(hit0, 1.0, jnp.where(hit1, 1.0, 0.0))
+            rank = dot_nn(named.astype(BF16), earlier)
+            rank_s[p] = jnp.where(named > 0.5, rank, -1.0)
+            return carry
+
+        lax.fori_loop(0, packs, prepare, 0)
+
+    def rows(p, carry):
+        here = pl.ds(pl.multiple_of(p * cap, cap), cap)
+        rank = rank_s[p, pl.ds(expert, 1), :]
+        gate_row = gate_s[p, pl.ds(expert, 1), :]
+        pick = iota((cap, length), 0).astype(F32) == rank
+        chosen = jnp.where(pick, 1.0, 0.0).astype(BF16)
+        taken = dot_nn(chosen, both_s[p])
+        gate_col = jnp.sum(jnp.where(pick, gate_row, 0.0), axis=1, keepdims=True)
+        x = taken[:, :width].astype(BF16)
+        g = taken[:, width:]
+        x_s[here, :] = x
+        grad_out = (gate_col * g).astype(BF16)
+        go_s[here, :] = grad_out
+        gate = dot_nn(x, inner_w[0, :, :hidden_width])
+        up = dot_nn(x, inner_w[0, :, hidden_width:])
+        sigma = 1.0 / (1.0 + jnp.exp(-gate))
+        active = gate * sigma
+        hidden = (active * up).astype(BF16)
+        hid_s[here, :] = hidden
+        result = dot_nn(hidden, down_w[0]).astype(BF16).astype(F32)
+        spot = pl.ds(pl.multiple_of(expert * cap, cap), cap)
+        y_s[p, spot, :width] = (gate_col * result).astype(BF16)
+        grad_gate = jnp.sum(g * result, axis=1, keepdims=True)
+        gg_s[p, pl.ds(expert, 1), :] = jnp.sum(jnp.where(pick, grad_gate, 0.0), axis=0, keepdims=True)
+        grad_hidden = dot_nt(grad_out, down_w[0])
+        gb_s[here, :hidden_width] = (grad_hidden * up * sigma * (1.0 + gate * (1.0 - sigma))).astype(BF16)
+        gb_s[here, hidden_width:] = (grad_hidden * active).astype(BF16)
+        y_s[p, spot, width:] = dot_nt(gb_s[here, :], inner_w[0]).astype(BF16)
+        return carry
+
+    lax.fori_loop(0, packs, rows, 0)
+    inner_g[0] = dot_tn(x_s[...], gb_s[...]).astype(BF16)
+    down_g[0] = dot_tn(hid_s[...], go_s[...]).astype(BF16)
+
+    @pl.when(expert == experts - 1)
+    def _():
+        def finish(p, carry):
+            ranks = rank_s[p].T
+            slot = iota((length, cap), 1).astype(F32)
+            pieces = [
+                jnp.where(ranks[:, e : e + 1] == slot, 1.0, 0.0).astype(BF16) for e in range(experts)
+            ]
+            back = dot_nn(jnp.concatenate(pieces, axis=1), y_s[p])
+            number = iota((experts, length), 0)
+            gate = gate_s[p]
+            grad_gate = gg_s[p]
+            mean = jnp.sum(gate * grad_gate, axis=0, keepdims=True)
+            hit = rank_s[p] > -0.5
+            grad_logits = jnp.where(hit, gate * (grad_gate - mean), 0.0).astype(BF16)
+            glog_o[p] = grad_logits
+            back_o[p, :, :width] = back[:, :width]
+            back_o[p, :, width:] = back[:, width:] + dot_tn(grad_logits, router_w[...])
+            return carry
+
+        lax.fori_loop(0, packs, finish, 0)
+
+
+def return_kernel(
+    patches, upstream, items, qkv_w, proj_w, gains, table, mixed, probs, att, mid, nm, back, glog,
+    block_o, patch_o, attn_g, small_g,
+    normed_s, branch_s, datt_s, dmix_s, dkv_s,
+):
+    packs, length, width = patches.shape
+    pairs = width // 128
+    experts = glog.shape[1]
+    low_lane = iota((1, width), 1) % HEAD < HEAD // 2
+    first_head = iota((1, 128), 1) < HEAD
+    mask_a = jnp.where(first_head, 1.0, 0.0).astype(BF16)
+    mask_b = jnp.where(first_head, 0.0, 1.0).astype(BF16)
+    top_rows = iota((128, 1), 0) < HEAD
+    small_g[...] = jnp.zeros(small_g.shape, F32)
+
+    def pack(p, carry):
+        rows = pl.ds(pl.multiple_of(p * length, length), length)
+        source = patches[p].astype(F32)
+        gain0, gain1 = gains[0:1, :], gains[1:2, :]
+        middle = mid[p]
+        inv = row_norm(middle)
+        unit = middle * inv
+        block_o[p] = (middle + back[p, :, :width]).astype(BF16)
+        grad_mid = back[p, :, width:]
+        small_g[experts : experts + 1, :] += jnp.zeros((1, width), F32)
+        small_g[experts + 1 : experts + 2, :] += jnp.sum(grad_mid * unit, axis=0, keepdims=True)
+        small_g[0:experts, :] += dot_nn(glog[p], nm[p])
+        grad_unit = grad_mid * gain1
+        grad_middle = upstream[p].astype(F32) + inv * (
+            grad_unit - unit * jnp.mean(grad_unit * unit, axis=1, keepdims=True)
+        )
+        patch_o[p] = grad_middle
+        branch = grad_middle.astype(BF16)
+        branch_s[rows, :] = branch
+        datt_s[...] = dot_nt(branch, proj_w[...]).astype(BF16)
+        dkv_s[...] = jnp.zeros(dkv_s.shape, F32)
+        item_row = items[p].astype(F32)
+        item_col, offset = positions(item_row, length)
+        cos_row, sin_row = rope_rows(offset, table[...], length, width)
+        for pair in range(pairs):
+            lanes = slice(128 * pair, 128 * pair + 128)
+            key_lanes = slice(width + 128 * pair, width + 128 * pair + 128)
+            value_lanes = slice(2 * width + 128 * pair, 2 * width + 128 * pair + 128)
+            keys_t = mixed[p, :, key_lanes].astype(F32).T.astype(BF16)
+            for block, (start, low, high) in enumerate(windows(length)):
+                query = mixed[p, start : start + QB, lanes] * 0.125
+                query = jnp.concatenate([query * mask_a, query * mask_b], axis=0)
+                datt = datt_s[start : start + QB, lanes]
+                datt = jnp.concatenate([datt * mask_a, datt * mask_b], axis=0)
+                prob = probs[p, pair, block, : high - low]
+                dprob = dot_nt(mixed[p, low:high, value_lanes], datt)
+                weight = prob.astype(F32)
+                mean = jnp.sum(weight * dprob, axis=0, keepdims=True)
+                dscore = (weight * (dprob - mean)).astype(BF16)
+                dkv_s[low:high, key_lanes] += dot_nn(dscore, query)
+                dkv_s[low:high, value_lanes] += dot_nn(prob, datt)
+                dquery = dot_nn(keys_t[:, low:high], dscore)
+                dquery = jnp.where(top_rows, dquery[:, :QB], dquery[:, QB:])
+                dkv_s[start : start + QB, lanes] = dquery.T * 0.125
+        dmix_s[rows, :width] = turn(dkv_s[:, :width], cos_row, -sin_row, low_lane).astype(BF16)
+        dmix_s[rows, width : 2 * width] = turn(
+            dkv_s[:, width : 2 * width], cos_row, -sin_row, low_lane
+        ).astype(BF16)
+        dmix_s[rows, 2 * width :] = dkv_s[:, 2 * width :].astype(BF16)
+        grad_normed = dot_nt(dmix_s[rows, :], qkv_w[...])
+        inv_in = row_norm(source)
+        unit_in = source * inv_in
+        normed_s[rows, :] = (unit_in * gain0).astype(BF16)
+        small_g[experts : experts + 1, :] += jnp.sum(grad_normed * unit_in, axis=0, keepdims=True)
+        grad_unit_in = grad_normed * gain0
+        patch_o[p] += inv_in * (
+            grad_unit_in - unit_in * jnp.mean(grad_unit_in * unit_in, axis=1, keepdims=True)
+        )
+        return carry
+
+    lax.fori_loop(0, packs, pack, 0)
+    attn_g[:, : 3 * width] = dot_tn(normed_s[...], dmix_s[...])
+    for p in range(packs):
+        pass
+    flat = jnp.concatenate([att[p] for p in range(packs)], axis=0)
+    attn_g[:, 3 * width :] = dot_tn(flat, branch_s[...])
+
+
+def whole(count):
+    return [pl.BlockSpec(memory_space=pltpu.VMEM)] * count
+
+
+LIMIT = pltpu.CompilerParams(vmem_limit_bytes=60 * 1024 * 1024)
+
+
+def run_attend(patches, items, qkv_w, proj_w, gains, table):
+    packs, length, width = patches.shape
+    pairs = width // 128
+    blocks = length // QB
+    shapes = (
+        jax.ShapeDtypeStruct((packs, length, 3 * width), BF16),
+        jax.ShapeDtypeStruct((packs, pairs, blocks, 3 * QB, 2 * QB), BF16),
+        jax.ShapeDtypeStruct((packs, length, width), BF16),
+        jax.ShapeDtypeStruct((packs, length, width), F32),
+        jax.ShapeDtypeStruct((packs, length, width), BF16),
+    )
+    return pl.pallas_call(
+        attend_kernel,
+        out_shape=shapes,
+        in_specs=whole(6),
+        out_specs=tuple(whole(5)),
+        compiler_params=LIMIT,
+        name="attend",
+    )(patches, items, qkv_w, proj_w, gains, table)
+
+
+def run_experts(nm, upstream, ids, router_w, inner_w, down_w):
+    packs, length, width = nm.shape
+    experts = router_w.shape[0]
+    hidden = down_w.shape[1]
+    cap = 2 * length * 2 // experts
+    fixed3 = lambda e: (0, 0, 0)
+    each = lambda e: (e, 0, 0)
+    grid_spec = pltpu.PrefetchScalarGridSpec(
+        num_scalar_prefetch=0,
+        grid=(experts,),
+        in_specs=[
+            pl.BlockSpec((packs, length, width), fixed3),
+            pl.BlockSpec((packs, length, width), fixed3),
+            pl.BlockSpec((packs, 2, length), fixed3),
+            pl.BlockSpec((experts, width), lambda e: (0, 0)),
+            pl.BlockSpec((1, width, 2 * hidden), each),
+            pl.BlockSpec((1, hidden, width), each),
+        ],
+        out_specs=(
+            pl.BlockSpec((1, width, 2 * hidden), each),
+            pl.BlockSpec((1, hidden, width), each),
+            pl.BlockSpec((packs, length, 2 * width), fixed3),
+            pl.BlockSpec((packs, experts, length), fixed3),
+        ),
+        scratch_shapes=[
+            pltpu.VMEM((packs, length, 2 * width), BF16),
+            pltpu.VMEM((packs, experts, length), F32),
+            pltpu.VMEM((packs, experts, length), F32),
+            pltpu.VMEM((packs, experts, length), F32),
+            pltpu.VMEM((packs * cap, width), BF16),
+            pltpu.VMEM((packs * cap, hidden), BF16),
+            pltpu.VMEM((packs * cap, width), BF16),
+            pltpu.VMEM((packs * cap, 2 * hidden), BF16),
+            pltpu.VMEM((packs, experts * cap, 2 * width), BF16),
+        ],
+    )
+    return pl.pallas_call(
+        expert_kernel,
+        out_shape=(
+            jax.ShapeDtypeStruct((experts, width, 2 * hidden), BF16),
+            jax.ShapeDtypeStruct((experts, hidden, width), BF16),
+            jax.ShapeDtypeStruct((packs, length, 2 * width), F32),
+            jax.ShapeDtypeStruct((packs, experts, length), BF16),
+        ),
+        grid_spec=grid_spec,
+        compiler_params=LIMIT,
+        name="experts",
+    )(nm, upstream, ids, router_w, inner_w, down_w)
+
+
+def run_return(patches, upstream, items, qkv_w, proj_w, gains, table, mixed, probs, att, mid, nm, back, glog):
+    packs, length, width = patches.shape
+    shapes = (
+        jax.ShapeDtypeStruct((packs, length, width), BF16),
+        jax.ShapeDtypeStruct((packs, length, width), F32),
+        jax.ShapeDtypeStruct((width, 4 * width), F32),
+        jax.ShapeDtypeStruct((16, width), F32),
+    )
+    return pl.pallas_call(
+        return_kernel,
+        out_shape=shapes,
+        in_specs=whole(14),
+        out_specs=tuple(whole(4)),
+        scratch_shapes=[
+            pltpu.VMEM((packs * length, width), BF16),
+            pltpu.VMEM((packs * length, width), BF16),
+            pltpu.VMEM((length, width), BF16),
+            pltpu.VMEM((packs * length, 3 * width), BF16),
+            pltpu.VMEM((length, 3 * width), F32),
+        ],
+        compiler_params=LIMIT,
+        name="backward",
+    )(patches, upstream, items, qkv_w, proj_w, gains, table, mixed, probs, att, mid, nm, back, glog)
+
+
+def fast(
+    patches, out_grad, item_ids, expert_ids,
+    qkv_master, qkv_first, qkv_second,
+    proj_master, proj_first, proj_second,
+    router_master, router_first, router_second,
+    gains_master, gains_first, gains_second,
+    inner_master, inner_first, inner_second,
+    down_master, down_first, down_second,
+):
+    width = patches.shape[2]
+    experts = router_master.shape[1]
+    inner_w = lax.all_gather(inner_master.astype(BF16), "dp", axis=1, tiled=True)
+    inner_w = lax.all_gather(inner_w, "expert", axis=0, tiled=True)
+    down_w = lax.all_gather(down_master.astype(BF16), "dp", axis=1, tiled=True)
+    down_w = lax.all_gather(down_w, "expert", axis=0, tiled=True)
+    qkv_w = qkv_master.astype(BF16)
+    proj_w = proj_master.astype(BF16)
+    router_w = router_master.T.astype(BF16)
+    ids = jnp.swapaxes(expert_ids, 1, 2)
+    table = jnp.asarray(rope_table(QB))
+    mixed, probs, att, mid, nm = run_attend(patches, item_ids, qkv_w, proj_w, gains_master, table)
+    inner_g, down_g, back, glog = run_experts(nm, out_grad, ids, router_w, inner_w, down_w)
+    block_out, patch_grad, attn_g, small_g = run_return(
+        patches, out_grad, item_ids, qkv_w, proj_w, gains_master, table, mixed, probs, att, mid, nm, back, glog
+    )
+    grad_inner = lax.psum_scatter(inner_g, "expert", scatter_dimension=0, tiled=True)
+    grad_inner = lax.psum_scatter(grad_inner, "dp", scatter_dimension=1, tiled=True).astype(F32)
+    grad_down = lax.psum_scatter(down_g, "expert", scatter_dimension=0, tiled=True)
+    grad_down = lax.psum_scatter(grad_down, "dp", scatter_dimension=1, tiled=True).astype(F32)
+    attn_g, small_g = lax.psum((attn_g, small_g), ("dp", "expert"))
+    qkv_new = adamw(qkv_master, qkv_first, qkv_second, attn_g[:, : 3 * width], 0.1, 0.1)
+    proj_new = adamw(proj_master, proj_first, proj_second, attn_g[:, 3 * width :], 0.4, 0.1)
+    router_new = adamw(router_master, router_first, router_second, small_g[:experts].T, 0.07, 0.1)
+    gains_new = adamw(gains_master, gains_first, gains_second, small_g[experts : experts + 2], 0.4, 0.0)
+    inner_new = adamw(inner_master, inner_first, inner_second, grad_inner, 0.1, 0.1)
+    down_new = adamw(down_master, down_first, down_second, grad_down, 0.15, 0.1)
+    return (block_out, patch_grad) + qkv_new + proj_new + router_new + gains_new + inner_new + down_new
+
+
+GATHER_LIMIT = 16 * 1024 * 1024
+
+
+def step(*args):
+    inner_master, down_master = args[16], args[19]
+    experts = inner_master.shape[0] * lax.axis_size("expert")
+    entries = inner_master.shape[1] * inner_master.shape[2] + down_master.shape[1] * down_master.shape[2]
+    weight_bytes = 2 * experts * entries * lax.axis_size("dp")
+    return (fast if weight_bytes <= GATHER_LIMIT else local)(*args)
+
+
 def solution(mesh):
     in_specs = (
         P(None, ("dp", "expert"), None),
@@ -357,4 +809,4 @@
         P("expert", "dp", None),
         P("expert", "dp", None),
     )
-    return jax.shard_map(local, mesh=mesh, in_specs=in_specs, out_specs=out_specs, check_vma=False)
+    return jax.shard_map(step, mesh=mesh, in_specs=in_specs, out_specs=out_specs, check_vma=False)

time: 991 us -> 780 us (0.79)
  matrix products: 177 us -> 0 us
  waiting for transfers between devices: 396 us -> 570 us
  local copies, waits for them, and re-layouts: 167 us -> 0.06 us
  Pallas kernels: 0 us -> 125 us
  other arithmetic: 127 us -> 19.8 us
  starting transfers between devices: 50.8 us -> 0.5 us
    all_to_all x12 -> x0, waiting for transfers between devices: 243 us -> none  [the longest x3 88.8 us: expert_forward(): lax.all_to_all(result, 'expert', split_axis=0, concat_axis=0, tiled=True)]
    reduce_scatter x2 -> x4, waiting for transfers between devices: 52.2 us -> 269 us  [the longest x1 165 us: fast(): lax.psum_scatter(inner_g, 'expert', scatter_dimension=0, tiled=True)]
    all_gather x1 -> x3, waiting for transfers between devices: 6.55 us -> 203 us  [the longest x1 138 us: fast(): inner_w = lax.all_gather(inner_w, 'expert', axis=0, tiled=True)]
    dot_general x63 -> x0, matrix products: 177 us -> none  [the longest x3 29.2 us: expert_forward(): jnp.einsum('sjcd,jdf->sjcf', grid, inner_low, preferred_element_type=jnp....]
    pallas_call x0 -> x3, Pallas kernels: none -> 125 us  [the longest x1 68.7 us: run_experts(): pl.pallas_call(expert_kernel, out_shape=(jax.ShapeDtypeStruct((experts, w...]
    all_to_all x12 -> x0, starting transfers between devices: 50.6 us -> none  [the longest x3 15.5 us: micro_step(): lax.all_to_all(outgoing, 'expert', split_axis=0, concat_axis=0, tiled=True)]
    gather x15 -> x0, local copies, waits for them, and re-layouts: 48.3 us -> none  [the longest x9 20.7 us: micro_step(): chosen = jnp.take_along_axis(logits, routes, axis=1)]
    reduce_sum x24 -> x0, other arithmetic: 38.6 us -> none  [the longest x3 17.3 us: micro_step(): combined = jnp.sum(gates[:, :, None] * picked, axis=1)]
  transfers between devices with their start and end apart: 16 -> 8, of which waited for: 16 -> 8; matrix products, arithmetic and copies ran while one was open for 22% -> 2% of each run, Pallas kernels for 0% -> 7%
where the time goes in v1:
time: 780 us; the launch traced here: 779 us
  waiting for transfers between devices  570 us (73%)
  Pallas kernels  125 us (16%)
  blocking collectives  49.9 us (6%)
  other arithmetic  19.8 us (3%)
  between operations  14.2 us (2%)
    reduce_scatter x1, waiting for transfers between devices, fast(): lax.psum_scatter(inner_g, 'expert', scatter_dimension=0, tiled=True)  165 us
    all_gather x1, waiting for transfers between devices, fast(): inner_w = lax.all_gather(inner_w, 'expert', axis=0, tiled=True)  138 us
    psum x1, waiting for transfers between devices, fast(): attn_g, small_g = lax.psum((attn_g, small_g), ('dp', 'expert'))  97.5 us
    pallas_call x1, Pallas kernels, run_experts(): pl.pallas_call(expert_kernel, out_shape=(jax.ShapeDtypeStruct((experts, w...  68.7 us
    reduce_scatter x1, waiting for transfers between devices, fast(): lax.psum_scatter(down_g, 'expert', scatter_dimension=0, tiled=True)  61.7 us
    all_gather x1, waiting for transfers between devices, fast(): down_w = lax.all_gather(down_w, 'expert', axis=0, tiled=True)  54.2 us
    psum x1, blocking collectives, fast(): attn_g, small_g = lax.psum((attn_g, small_g), ('dp', 'expert'))  40.4 us
    pallas_call x1, Pallas kernels, run_return(): pl.pallas_call(return_kernel, out_shape=shapes, in_specs=whole(14), out_s...  31.4 us
  transfers between devices with their start and end apart: 8, of which 8 were waited for; matrix products, arithmetic and copies ran while one was open for 2% of the time, Pallas kernels for 7%

profile of v1, /device:TPU:0, one launch (start us, length us, event | category | flops | bytes accessed | tf_op | source)
XLA Modules:
  0.0 779.5 jit_solution(7499700044682806881)
XLA Ops:
  7.2 1.8 convert_element_type.27
  9.1 1.0 convert_element_type.28
  10.2 9.6 %all_gather.14 = bf16[1,768,384]{2,1,0:T(8,128)(2,1)} all-gather(bf16[1,192,384]{2,1,0:T(8,128)(2,1)S(1)} %convert_element_type.28), channel_id=1, replica_groups=mesh['dp'=4,'expert'=8] {'dp'}, dimensions={1}, use_global_device_ids=true | all-gather | bytes 737280 | tf_op jit(solution)/shard_map/all_gather | solution.py:728
  19.8 10.5 %all-gather.4.cloned.1.call-done = bf16[1,384,1536]{2,1,0:T(8,128)(2,1)} async-done(((bf16[1,96,1536]{2,1,0:T(8,128)(2,1)}), bf16[1,384,1536]{2,1,0:T(8,128)(2,1)}) %all-gather.4.cloned.1.call-update) | async-done | bytes 1179664 | tf_op jit(solution)/shard_map/all_gather | solution.py:726
  30.4 0.7 convert_element_type.24.proj_w
  31.2 1.0 convert_element_type.23.qkv_w
  32.2 24.9 %attend.1 = (bf16[3,512,1152]{2,1,0:T(8,128)(2,1)}, bf16[3,3,4,384,256]{4,3,2,1,0:T(8,128)(2,1)}, bf16[3,512,384]{2,1,0:T(8,128)(2,1)}, f32[3,512,384]{2,1,0:T(8,128)}, bf16[3,512,384]{2,1,0:T(8,128)(2,1)}) custom-call(bf16[3,512,384]{2,1,0:T(8,128)(2,1)} %patches.3, s32[3,1,512]{2,1,0:T(1,128)} %items.3, bf16[384,1152]{1,0:T(8,128)(2,1)} %convert_element_type.23.qkv_w, ...), custom_call_target="tpu_custom_call" | custom-call | tf_op jit(solution)/shard_map/attend/pallas_call | solution.py:630
  57.0 0.6 convert_bitcast_fusion.router_w
  57.6 54.2 %all-gather.8.cloned.1.call-done.down_w = bf16[8,768,384]{2,1,0:T(8,128)(2,1)} async-done(((bf16[1,768,384]{2,1,0:T(8,128)(2,1)}), bf16[8,768,384]{2,1,0:T(8,128)(2,1)}) %all-gather.8.cloned.1.call-update) | async-done | bytes 4718608 | tf_op jit(solution)/shard_map/all_gather | solution.py:729
  111.9 137.8 %all-gather.6.cloned.1.call-done.inner_w = bf16[8,384,1536]{2,1,0:T(8,128)(2,1)} async-done(((bf16[1,384,1536]{2,1,0:T(8,128)(2,1)}), bf16[8,384,1536]{2,1,0:T(8,128)(2,1)}) %all-gather.6.cloned.1.call-update) | async-done | bytes 9437200 | tf_op jit(solution)/shard_map/all_gather | solution.py:727
  249.7 68.7 %experts.1 = (bf16[8,384,1536]{2,1,0:T(8,128)(2,1)}, bf16[8,768,384]{2,1,0:T(8,128)(2,1)}, f32[3,512,768]{2,1,0:T(8,128)}, bf16[3,8,512]{2,1,0:T(8,128)(2,1)}) custom-call(bf16[3,512,384]{2,1,0:T(8,128)(2,1)} %get-tuple-element.37.nm, bf16[3,512,384]{2,1,0:T(8,128)(2,1)} %upstream.3, s32[3,2,512]{2,1,0:T(2,128)} %bitcast.11, ...), custom_call_target="tpu_custom_call" | custom-call | tf_op jit(solution)/shard_map/experts/pallas_call | solution.py:676
  319.3 31.4 %backward.1 = (bf16[3,512,384]{2,1,0:T(8,128)(2,1)}, f32[3,512,384]{2,1,0:T(8,128)}, f32[384,1536]{1,0:T(8,128)}, f32[16,384]{1,0:T(8,128)}) custom-call(bf16[3,512,384]{2,1,0:T(8,128)(2,1)} %patches.3, bf16[3,512,384]{2,1,0:T(8,128)(2,1)} %upstream.3, s32[3,1,512]{2,1,0:T(1,128)} %items.3, bf16[384,1152]{1,0:T(8,128)(2,1)} %convert_element_type.23.qkv_w, ...), custom_call_target="tpu_custom_call" | custom-call | tf_op jit(solution)/shard_map/backward/pallas_call | solution.py:698
  350.8 61.7 %reduce-scatter.9.cloned.1.call-done = bf16[1,768,384]{2,1,0:T(8,128)(2,1)} async-done(((bf16[8,768,384]{2,1,0:T(8,128)(2,1)}), bf16[1,768,384]{2,1,0:T(8,128)(2,1)}) %reduce-scatter.9.cloned.1.call-update) | async-done | bytes 589840 | tf_op jit(solution)/shard_map/reduce_scatter | solution.py:742
  412.5 165.2 %reduce-scatter.5.cloned.1.call-done = bf16[1,384,1536]{2,1,0:T(8,128)(2,1)} async-done(((bf16[8,384,1536]{2,1,0:T(8,128)(2,1)}), bf16[1,384,1536]{2,1,0:T(8,128)(2,1)}) %reduce-scatter.5.cloned.1.call-update) | async-done | bytes 1179664 | tf_op jit(solution)/shard_map/reduce_scatter | solution.py:740
  577.7 40.4 %psum.15 = f32[16,384]{1,0:T(8,128)} all-reduce(f32[16,384]{1,0:T(8,128)} %get-tuple-element.43), channel_id=1, replica_groups=mesh['dp'=4,'expert'=8] {'dp','expert'}, use_global_device_ids=true, to_apply=%region_1.0 | all-reduce | flops 6144 | bytes 49152 | tf_op jit(solution)/shard_map/psum | solution.py:744
  618.1 1.3 multiply_subtract_fusion.5
  619.4 1.4 multiply_subtract_fusion.4
  620.8 97.5 %all-reduce.2.cloned.1.call-done = f32[384,1536]{1,0:T(8,128)} async-done(((f32[384,1536]{1,0:T(8,128)}), f32[384,1536]{1,0:T(8,128)}) %all-reduce.2.cloned.1.call-update) | async-done | bytes 2359312 | tf_op jit(solution)/shard_map/psum | solution.py:744
  718.3 2.7 multiply_subtract_fusion.2
  721.1 4.9 multiply_subtract_fusion
  726.0 16.0 %reduce-scatter.11.cloned.1.call-done = bf16[1,192,384]{2,1,0:T(8,128)(2,1)} async-done(((bf16[1,768,384]{2,1,0:T(8,128)(2,1)}), bf16[1,192,384]{2,1,0:T(8,128)(2,1)}) %reduce-scatter.11.cloned.1.call-update) | async-done | bytes 147472 | tf_op jit(solution)/shard_map/reduce_scatter | solution.py:743
  742.0 1.9 multiply_subtract_fusion.3
  744.0 26.2 %reduce-scatter.7.cloned.1.call-done = bf16[1,96,1536]{2,1,0:T(8,128)(2,1)} async-done(((bf16[1,384,1536]{2,1,0:T(8,128)(2,1)}), bf16[1,96,1536]{2,1,0:T(8,128)(2,1)}) %reduce-scatter.7.cloned.1.call-update) | async-done | bytes 294928 | tf_op jit(solution)/shard_map/reduce_scatter | solution.py:741
  770.2 2.4 multiply_subtract_fusion.1
  (44 shorter events, 1.2 us)
Async XLA Ops:
  7.2 23.1 %all-gather.4.cloned.1.call-start = ((), (), s32[]{:S(2)}) async-start(), calls=%async_computation.4 | async-start | bytes 1474560 | tf_op jit(solution)/shard_map/all_gather | solution.py:726
  9.0 21.3 %copy-start.2 = (f32[384,384]{1,0:T(8,128)S(1)}, f32[384,384]{1,0:T(8,128)}, u32[]{:S(2)}) copy-start(f32[384,384]{1,0:T(8,128)} %param.30) | copy-start | bytes 1769476
  9.1 102.8 %all-gather.8.cloned.1.call-start = ((), (), s32[]{:S(2)}) async-start(), calls=%async_computation.6 | async-start | bytes 5308416 | tf_op jit(solution)/shard_map/all_gather | solution.py:729
  10.2 21.0 %copy-start = (f32[384,1152]{1,0:T(8,128)S(1)}, f32[384,1152]{1,0:T(8,128)}, u32[]{:S(2)}) copy-start(f32[384,1152]{1,0:T(8,128)} %param.27) | copy-start | bytes 5308420
  19.8 229.9 %all-gather.6.cloned.1.call-start = ((), (), s32[]{:S(2)}) async-start(), calls=%async_computation.5 | async-start | bytes 10616832 | tf_op jit(solution)/shard_map/all_gather | solution.py:727
  30.3 382.1 %reduce-scatter.9.cloned.1.call-start = ((), (), s32[]{:S(2)}) async-start(), calls=%async_computation.10 | async-start | bytes 5308416 | tf_op jit(solution)/shard_map/reduce_scatter | solution.py:742
  32.2 24.9 %copy-start.12 = (f32[384,8]{0,1:T(8,128)S(1)}, f32[384,8]{0,1:T(8,128)}, u32[]{:S(2)}) copy-start(f32[384,8]{0,1:T(8,128)} %param.33) | copy-start | bytes 36868
  318.5 259.2 %reduce-scatter.5.cloned.1.call-start = ((), (), s32[]{:S(2)}) async-start(), calls=%async_computation.8 | async-start | bytes 10616832 | tf_op jit(solution)/shard_map/reduce_scatter | solution.py:740
  319.0 399.3 %all-reduce.2.cloned.1.call-start = ((), (), s32[]{:S(2)}) async-start(), calls=%async_computation.7 | async-start | bytes 4718592 | tf_op jit(solution)/shard_map/psum | solution.py:744
  350.7 267.4 %copy-start.13 = (f32[2,384]{1,0:T(2,128)S(1)}, f32[2,384]{1,0:T(2,128)}, u32[]{:S(2)}) copy-start(f32[2,384]{1,0:T(2,128)} %gains.3) | copy-start | bytes 9220
  350.7 367.6 %copy-start.6 = (f32[384,384]{1,0:T(8,128)S(1)}, f32[384,384]{1,0:T(8,128)}, u32[]{:S(2)}) copy-start(f32[384,384]{1,0:T(8,128)} %param.31) | copy-start | bytes 1769476
  350.7 367.6 %copy-start.7 = (f32[384,384]{1,0:T(8,128)S(1)}, f32[384,384]{1,0:T(8,128)}, u32[]{:S(2)}) copy-start(f32[384,384]{1,0:T(8,128)} %param.32) | copy-start | bytes 1769476
  350.7 391.3 %reduce-scatter.11.cloned.1.call-start = ((), (), s32[]{:S(2)}) async-start(), calls=%async_computation.11 | async-start | bytes 737280 | tf_op jit(solution)/shard_map/reduce_scatter | solution.py:743
  412.5 357.7 %reduce-scatter.7.cloned.1.call-start = ((), (), s32[]{:S(2)}) async-start(), calls=%async_computation.9 | async-start | bytes 1474560 | tf_op jit(solution)/shard_map/reduce_scatter | solution.py:741
  718.3 2.7 copy-start.1
  718.3 2.7 copy-start.4
  721.0 21.0 %copy-start.5 = (f32[1,192,384]{2,1,0:T(8,128)S(1)}, f32[1,192,384]{2,1,0:T(8,128)}, u32[]{:S(2)}) copy-start(f32[1,192,384]{2,1,0:T(8,128)} %param.42) | copy-start | bytes 884740
  721.0 21.0 %copy-start.10 = (f32[1,192,384]{2,1,0:T(8,128)S(1)}, f32[1,192,384]{2,1,0:T(8,128)}, u32[]{:S(2)}) copy-start(f32[1,192,384]{2,1,0:T(8,128)} %param.43) | copy-start | bytes 884740
  721.1 20.9 %copy-start.11 = (f32[1,192,384]{2,1,0:T(8,128)S(1)}, f32[1,192,384]{2,1,0:T(8,128)}, u32[]{:S(2)}) copy-start(f32[1,192,384]{2,1,0:T(8,128)} %param.44) | copy-start | bytes 884740
  725.9 44.2 %copy-start.3 = (f32[1,96,1536]{2,1,0:T(8,128)S(1)}, f32[1,96,1536]{2,1,0:T(8,128)}, u32[]{:S(2)}) copy-start(f32[1,96,1536]{2,1,0:T(8,128)} %param.39) | copy-start | bytes 1769476
  726.0 44.2 %copy-start.8 = (f32[1,96,1536]{2,1,0:T(8,128)S(1)}, f32[1,96,1536]{2,1,0:T(8,128)}, u32[]{:S(2)}) copy-start(f32[1,96,1536]{2,1,0:T(8,128)} %param.40) | copy-start | bytes 1769476
  726.0 44.2 %copy-start.9 = (f32[1,96,1536]{2,1,0:T(8,128)S(1)}, f32[1,96,1536]{2,1,0:T(8,128)}, u32[]{:S(2)}) copy-start(f32[1,96,1536]{2,1,0:T(8,128)} %param.41) | copy-start | bytes 1769476
Sparse Core Ops, SparseCore 0:
  10.1 20.1 all-gather.3
  32.5 79.3 all-gather.7
  114.1 135.5 all-gather.5
  318.6 93.8 reduce-scatter.8
  415.9 161.7 reduce-scatter.4
  583.1 135.1 all-reduce.1
  720.8 21.1 reduce-scatter.10
  744.6 25.5 reduce-scatter.6

commit v2 on v1

--- a/solution.py
+++ b/solution.py
@@ -1,3 +1,5 @@
+import functools
+
 import jax
 import jax.numpy as jnp
 import numpy as np
@@ -433,14 +435,25 @@
     lax.fori_loop(0, packs, pack, 0)
 
 
+def unpack(weights, inner_w, down_w):
+    copies, width = weights.shape[1], inner_w.shape[0]
+    deep, span = width // copies, down_w.shape[0] // copies
+    for d in range(copies):
+        for block in range(inner_w.shape[1] // width):
+            inner_w[d * deep : d * deep + deep, block * width : block * width + width] = weights[
+                0, d, block * deep : block * deep + deep, :
+            ]
+        down_w[d * span : d * span + span, :] = weights[0, d, width:, :]
+
+
 def expert_kernel(
-    nm, upstream, ids, router_w, inner_w, down_w,
-    inner_g, down_g, back_o, glog_o,
-    both_s, rank_s, gate_s, gg_s, x_s, hid_s, go_s, gb_s, y_s,
+    nm, upstream, ids, router_w, weights,
+    part, back_o, glog_o,
+    both_s, rank_s, gate_s, gg_s, x_s, hid_s, go_s, gb_s, y_s, inner_w, down_w,
 ):
     packs, length, width = nm.shape
     experts = router_w.shape[0]
-    hidden_width = down_w.shape[1]
+    hidden_width = down_w.shape[0]
     cap = x_s.shape[0] // packs
     expert = pl.program_id(0)
 
@@ -469,6 +482,8 @@
 
         lax.fori_loop(0, packs, prepare, 0)
 
+    unpack(weights, inner_w, down_w)
+
     def rows(p, carry):
         here = pl.ds(pl.multiple_of(p * cap, cap), cap)
         rank = rank_s[p, pl.ds(expert, 1), :]
@@ -482,26 +497,34 @@
         x_s[here, :] = x
         grad_out = (gate_col * g).astype(BF16)
         go_s[here, :] = grad_out
-        gate = dot_nn(x, inner_w[0, :, :hidden_width])
-        up = dot_nn(x, inner_w[0, :, hidden_width:])
+        gate = dot_nn(x, inner_w[:, :hidden_width])
+        up = dot_nn(x, inner_w[:, hidden_width:])
         sigma = 1.0 / (1.0 + jnp.exp(-gate))
         active = gate * sigma
         hidden = (active * up).astype(BF16)
         hid_s[here, :] = hidden
-        result = dot_nn(hidden, down_w[0]).astype(BF16).astype(F32)
+        result = dot_nn(hidden, down_w[...]).astype(BF16).astype(F32)
         spot = pl.ds(pl.multiple_of(expert * cap, cap), cap)
         y_s[p, spot, :width] = (gate_col * result).astype(BF16)
         grad_gate = jnp.sum(g * result, axis=1, keepdims=True)
         gg_s[p, pl.ds(expert, 1), :] = jnp.sum(jnp.where(pick, grad_gate, 0.0), axis=0, keepdims=True)
-        grad_hidden = dot_nt(grad_out, down_w[0])
+        grad_hidden = dot_nt(grad_out, down_w[...])
         gb_s[here, :hidden_width] = (grad_hidden * up * sigma * (1.0 + gate * (1.0 - sigma))).astype(BF16)
         gb_s[here, hidden_width:] = (grad_hidden * active).astype(BF16)
-        y_s[p, spot, width:] = dot_nt(gb_s[here, :], inner_w[0]).astype(BF16)
+        y_s[p, spot, width:] = dot_nt(gb_s[here, :], inner_w[...]).astype(BF16)
         return carry
 
     lax.fori_loop(0, packs, rows, 0)
-    inner_g[0] = dot_tn(x_s[...], gb_s[...]).astype(BF16)
-    down_g[0] = dot_tn(hid_s[...], go_s[...]).astype(BF16)
+    copies = part.shape[1]
+    deep, span = width // copies, hidden_width // copies
+    for block in range(2 * hidden_width // width):
+        lanes = slice(block * width, block * width + width)
+        grad = dot_tn(x_s[...], gb_s[:, lanes]).astype(BF16)
+        for d in range(copies):
+            part[0, d, block * deep : block * deep + deep, :] = grad[d * deep : d * deep + deep]
+    grad = dot_tn(hid_s[...], go_s[...]).astype(BF16)
+    for d in range(copies):
+        part[0, d, width:, :] = grad[d * span : d * span + span]
 
     @pl.when(expert == experts - 1)
     def _():
@@ -528,8 +551,8 @@
 
 def return_kernel(
     patches, upstream, items, qkv_w, proj_w, gains, table, mixed, probs, att, mid, nm, back, glog,
-    block_o, patch_o, attn_g, small_g,
-    normed_s, branch_s, datt_s, dmix_s, dkv_s,
+    block_o, patch_o, tail_o,
+    normed_s, branch_s, datt_s, dmix_s, dkv_s, small_g,
 ):
     packs, length, width = patches.shape
     pairs = width // 128
@@ -602,11 +625,427 @@
         return carry
 
     lax.fori_loop(0, packs, pack, 0)
-    attn_g[:, : 3 * width] = dot_tn(normed_s[...], dmix_s[...])
-    for p in range(packs):
-        pass
     flat = jnp.concatenate([att[p] for p in range(packs)], axis=0)
-    attn_g[:, 3 * width :] = dot_tn(flat, branch_s[...])
+    tail_o[...] = jnp.zeros(tail_o.shape, BF16)
+    for block in range(4):
+        if block < 3:
+            grad = dot_tn(normed_s[...], dmix_s[:, block * width : block * width + width])
+        else:
+            grad = dot_tn(flat, branch_s[...])
+        lay_tail(tail_o, block, grad.astype(BF16))
+    tail_o[0, 0, tail_o.shape[2] - 16 :, :] = small_g[...].astype(BF16)
+
+
+def tail_rows(width, devices):
+    return 4 * width // devices + 16
+
+
+def lay_tail(tail, block, grad):
+    ex, dp, rows, width = tail.shape
+    rows = rows - 16
+    each = width // rows
+    for piece in range(each):
+        number = block * each + piece
+        tail[number // dp, number % dp, :rows, :] = grad[piece * rows : piece * rows + rows]
+
+
+MESH_ID = pl.DeviceIdType.MESH
+
+
+class Place:
+    def __init__(self, line):
+        self.line = line
+        dp, ex = lax.axis_index("dp"), lax.axis_index("expert")
+        self.x, self.core = lax.div(dp, 2), lax.rem(dp, 2)
+        self.z, self.y = lax.div(ex, 2), lax.rem(ex, 2)
+
+    def device(self, flip_x=0, flip_y=0, flip_core=0, z=None):
+        x = 1 - self.x if flip_x else self.x
+        y = 1 - self.y if flip_y else self.y
+        core = 1 - self.core if flip_core else self.core
+        return (2 * x + core, 2 * (self.z if z is None else z) + y)
+
+    def levels(self):
+        found = [(0, self.z, None)]
+        for away in range(1, self.line):
+            found.append((away, self.z - away, self.z >= away))
+            found.append((away, self.z + away, self.z + away < self.line))
+        return found
+
+    def greet(self):
+        barrier = pltpu.get_barrier_semaphore()
+
+        def signal(device):
+            pl.semaphore_signal(barrier, inc=1, device_id=device, device_id_type=MESH_ID)
+
+        for device in (self.device(1), self.device(0, 1), self.device(0, 0, 1)):
+            signal(device)
+        pl.when(self.z > 0)(lambda: signal(self.device(z=self.z - 1)))
+        pl.when(self.z + 1 < self.line)(lambda: signal(self.device(z=self.z + 1)))
+        ends = (self.z == 0).astype(jnp.int32) + (self.z + 1 == self.line).astype(jnp.int32)
+        pl.semaphore_wait(barrier, 5 - ends)
+
+
+def both(*tests):
+    tests = [t for t in tests if t is not None]
+    if not tests:
+        return None
+    found = tests[0]
+    for t in tests[1:]:
+        found = jnp.logical_and(found, t)
+    return found
+
+
+def only(test, body):
+    if test is None:
+        body()
+    else:
+        pl.when(test)(body)
+
+
+class Wires:
+    def __init__(self, send_sem):
+        self.send_sem = send_sem
+        self.sent = []
+
+    def send(self, source, target, arrival, device, test=None):
+        copy = pltpu.make_async_remote_copy(
+            src_ref=source,
+            dst_ref=target,
+            send_sem=self.send_sem.at[len(self.sent)],
+            recv_sem=arrival,
+            device_id=device,
+            device_id_type=MESH_ID,
+        )
+        only(test, copy.start)
+        self.sent.append((copy, test))
+
+    def arrived(self, target, arrival, device, test=None):
+        copy = pltpu.make_async_remote_copy(
+            src_ref=target,
+            dst_ref=target,
+            send_sem=self.send_sem.at[0],
+            recv_sem=arrival,
+            device_id=device,
+            device_id_type=MESH_ID,
+        )
+        only(test, copy.wait_recv)
+
+    def finish(self):
+        for copy, test in self.sent:
+            only(test, copy.wait_send)
+
+
+class Gather:
+    def __init__(self, place, shard, full, send_sem, recv_sem, copy_sem):
+        self.place, self.shard, self.full = place, shard, full
+        self.recv_sem, self.copy_sem = recv_sem, copy_sem
+        self.wires = Wires(send_sem)
+
+    def at(self, device):
+        return self.full.at[device[1], device[0]]
+
+    def ready(self, device):
+        return self.recv_sem.at[device[1], device[0]]
+
+    def pass_on(self, origin, to, test=None, source=None):
+        source = self.at(origin) if source is None else source
+        self.wires.send(source, self.at(origin), self.ready(origin), to, test)
+
+    def wait(self, origin, test=None):
+        self.wires.arrived(self.at(origin), self.ready(origin), self.place.device(0, 0, 1), test)
+
+    def start(self):
+        place = self.place
+        me = place.device()
+        up, down = place.z + 1 < place.line, place.z > 0
+        self.pass_on(me, place.device(z=place.z + 1), up, self.shard)
+        self.pass_on(me, place.device(z=place.z - 1), down, self.shard)
+        self.pass_on(me, place.device(1), None, self.shard)
+        self.pass_on(me, place.device(0, 1), None, self.shard)
+        self.pass_on(me, place.device(0, 0, 1), None, self.shard)
+        self.own = pltpu.make_async_copy(self.shard, self.at(me), self.copy_sem)
+        self.own.start()
+
+    def column(self, away):
+        place = self.place
+        for dist, level, test in place.levels():
+            if dist != away:
+                continue
+            origin = place.device(z=level)
+            self.wait(origin, test)
+            if level is not place.z:
+                upward = jnp.logical_and(level < place.z, place.z + 1 < place.line)
+                downward = jnp.logical_and(level > place.z, place.z > 0)
+                self.pass_on(origin, place.device(z=place.z + 1), both(test, upward))
+                self.pass_on(origin, place.device(z=place.z - 1), both(test, downward))
+            self.pass_on(origin, place.device(1), test)
+            self.pass_on(origin, place.device(0, 1), test)
+            self.pass_on(origin, place.device(0, 0, 1), test)
+
+    def square(self, away):
+        place = self.place
+        for dist, level, test in place.levels():
+            if dist != away:
+                continue
+            over_x, over_y = place.device(1, z=level), place.device(0, 1, z=level)
+            self.wait(over_x, test)
+            if dist % 2 == 0:
+                self.pass_on(over_x, place.device(0, 1), test)
+            self.pass_on(over_x, place.device(0, 0, 1), test)
+            self.wait(over_y, test)
+            if dist % 2 == 1:
+                self.pass_on(over_y, place.device(1), test)
+            self.pass_on(over_y, place.device(0, 0, 1), test)
+
+    def corner(self, away):
+        place = self.place
+        for dist, level, test in place.levels():
+            if dist != away:
+                continue
+            across = place.device(1, 1, z=level)
+            self.wait(across, test)
+            self.pass_on(across, place.device(0, 0, 1), test)
+
+    def partner(self, flip_x, flip_y, away):
+        place = self.place
+        for dist, level, test in place.levels():
+            if dist == away:
+                self.wait(place.device(flip_x, flip_y, 1, z=level), test)
+
+
+def gather_kernel(line, shard, full, send_sem, recv_sem, copy_sem):
+    place = Place(line)
+    place.greet()
+    gather = Gather(place, shard, full, send_sem, recv_sem, copy_sem)
+    gather.start()
+    for away in range(1, line):
+        gather.column(away)
+        gather.square(away - 1)
+    gather.square(line - 1)
+    for away in range(line):
+        gather.corner(away)
+    for flip_x in range(2):
+        for flip_y in range(2):
+            for away in range(line):
+                gather.partner(flip_x, flip_y, away)
+    gather.own.wait()
+    gather.wires.finish()
+
+
+def run_gather(shard, slot):
+    rows, width = shard.shape
+    dp, ex = lax.axis_size("dp"), lax.axis_size("expert")
+    line = ex // 2
+    return pl.pallas_call(
+        functools.partial(gather_kernel, line),
+        out_shape=jax.ShapeDtypeStruct((ex, dp, rows, width), shard.dtype),
+        in_specs=[pl.BlockSpec(memory_space=pltpu.VMEM)],
+        out_specs=pl.BlockSpec(memory_space=pl.ANY),
+        scratch_shapes=[
+            pltpu.SemaphoreType.DMA((32 * line,)),
+            pltpu.SemaphoreType.DMA((ex, dp)),
+            pltpu.SemaphoreType.DMA,
+        ],
+        compiler_params=pltpu.CompilerParams(
+            collective_id=slot, has_side_effects=True, vmem_limit_bytes=60 * 1024 * 1024
+        ),
+        name="gather",
+    )(shard)
+
+
+OWN, OVER_X, OVER_Y, ACROSS = 0, 1, 2, 3
+FLIPS = ((0, 0), (1, 0), (0, 1), (1, 1))
+
+
+class Reduce:
+    def __init__(self, place, part, sums, core_in, diag_in, side_in, line_in, send_sem, recv, copy_sem):
+        self.place, self.part, self.sums = place, part, sums
+        self.core_in, self.diag_in, self.side_in, self.line_in = core_in, diag_in, side_in, line_in
+        self.core_sem, self.diag_sem, self.side_sem, self.line_sem = recv
+        self.copy_sem = copy_sem
+        self.wires = Wires(send_sem)
+        self.loads = []
+
+    def shard(self, group, level, flip_core=0):
+        device = self.place.device(*FLIPS[group], flip_core, z=level)
+        return self.part.at[device[1], device[0]]
+
+    def pick(self, away):
+        return [(level, test) for dist, level, test in self.place.levels() if dist == away]
+
+    def share(self, group, away):
+        for level, test in self.pick(away):
+            load = pltpu.make_async_copy(
+                self.shard(group, level), self.sums.at[group, level], self.copy_sem.at[group, level]
+            )
+            only(test, load.start)
+            self.wires.send(
+                self.shard(group, level, 1),
+                self.core_in.at[group, level],
+                self.core_sem.at[group, level],
+                self.place.device(0, 0, 1),
+                test,
+            )
+
+    def add(self, group, level, value):
+        self.sums[group, level] = (self.sums[group, level].astype(F32) + value.astype(F32)).astype(BF16)
+
+    def merge(self, group, away):
+        place = self.place
+        for level, test in self.pick(away):
+
+            def body(level=level):
+                pltpu.make_async_copy(
+                    self.shard(group, level), self.sums.at[group, level], self.copy_sem.at[group, level]
+                ).wait()
+                self.wires.arrived(
+                    self.core_in.at[group, level],
+                    self.core_sem.at[group, level],
+                    place.device(0, 0, 1),
+                )
+                self.add(group, level, self.core_in[group, level])
+
+            only(test, body)
+
+    def send_across(self, away):
+        place = self.place
+        side = OVER_Y if away % 2 == 0 else OVER_X
+        for level, test in self.pick(away):
+            self.wires.send(
+                self.sums.at[ACROSS, level],
+                self.diag_in.at[level],
+                self.diag_sem.at[level],
+                place.device(*FLIPS[side]),
+                test,
+            )
+
+    def send_side(self, away):
+        place = self.place
+        group = OVER_X if away % 2 == 0 else OVER_Y
+        for level, test in self.pick(away):
+
+            def body(level=level):
+                self.wires.arrived(self.diag_in.at[level], self.diag_sem.at[level], place.device(1))
+                self.add(group, level, self.diag_in[level])
+
+            only(test, body)
+            for side in (OVER_X, OVER_Y):
+                self.wires.send(
+                    self.sums.at[side, level],
+                    self.side_in.at[side - 1, level],
+                    self.side_sem.at[side - 1, level],
+                    place.device(*FLIPS[side]),
+                    test,
+                )
+
+    def collect(self, level, test):
+        place = self.place
+
+        def body():
+            total = self.sums[OWN, level].astype(F32)
+            for side in range(2):
+                self.wires.arrived(
+                    self.side_in.at[side, level], self.side_sem.at[side, level], place.device(1)
+                )
+                total = total + self.side_in[side, level].astype(F32)
+            self.sums[OWN, level] = total.astype(BF16)
+
+        only(test, body)
+
+    def send_line(self, away):
+        place = self.place
+        for level, test in self.pick(away):
+            self.collect(level, test)
+            below = level is not place.z and level < place.z
+            for way, test_way, far in (
+                (0, jnp.logical_and(test, level < place.z), place.z + 1 < place.line),
+                (1, jnp.logical_and(test, level > place.z), place.z > 0),
+            ):
+
+                def body(level=level, way=way):
+                    self.wires.arrived(
+                        self.line_in.at[way, level], self.line_sem.at[way, level], place.device(1)
+                    )
+                    self.add(OWN, level, self.line_in[way, level])
+
+                only(jnp.logical_and(test_way, far), body)
+                self.wires.send(
+                    self.sums.at[OWN, level],
+                    self.line_in.at[way, level],
+                    self.line_sem.at[way, level],
+                    place.device(z=place.z - 1 if way == 0 else place.z + 1),
+                    test_way,
+                )
+
+    def finish(self, out):
+        place = self.place
+        level = place.z
+        total = self.sums[OWN, level].astype(F32)
+        for side in range(2):
+            self.wires.arrived(
+                self.side_in.at[side, level], self.side_sem.at[side, level], place.device(1)
+            )
+            total = total + self.side_in[side, level].astype(F32)
+        out[...] = total
+        for way, far in ((0, place.z + 1 < place.line), (1, place.z > 0)):
+
+            def body(way=way):
+                self.wires.arrived(
+                    self.line_in.at[way, level], self.line_sem.at[way, level], place.device(1)
+                )
+                out[...] += self.line_in[way, level].astype(F32)
+
+            only(far, body)
+        self.wires.finish()
+
+
+def reduce_kernel(
+    line, part, out, sums, core_in, diag_in, side_in, line_in,
+    send_sem, core_sem, diag_sem, side_sem, line_sem, copy_sem,
+):
+    place = Place(line)
+    place.greet()
+    reduce = Reduce(
+        place, part, sums, core_in, diag_in, side_in, line_in,
+        send_sem, (core_sem, diag_sem, side_sem, line_sem), copy_sem,
+    )
+    order = list(range(line - 1, -1, -1))
+    for group in (ACROSS, OVER_X, OVER_Y, OWN):
+        for away in order:
+            reduce.share(group, away)
+    for away in order:
+        reduce.merge(ACROSS, away)
+        reduce.send_across(away)
+    for group in (OVER_X, OVER_Y, OWN):
+        for away in order:
+            reduce.merge(group, away)
+    for away in order:
+        reduce.send_side(away)
+    for away in order[:-1]:
+        reduce.send_line(away)
+    reduce.finish(out)
+
+
+def run_reduce(part, slot):
+    ex, dp, rows, width = part.shape
+    line = ex // 2
+    dma = pltpu.SemaphoreType.DMA
+    slab = lambda *dims: pltpu.VMEM(dims + (rows, width), part.dtype)
+    return pl.pallas_call(
+        functools.partial(reduce_kernel, line),
+        out_shape=jax.ShapeDtypeStruct((rows, width), F32),
+        in_specs=[pl.BlockSpec(memory_space=pl.ANY)],
+        out_specs=pl.BlockSpec(memory_space=pltpu.VMEM),
+        scratch_shapes=[
+            slab(4, line), slab(4, line), slab(line), slab(2, line), slab(2, line),
+            dma((32 * line,)), dma((4, line)), dma((line,)), dma((2, line)), dma((2, line)), dma((4, line)),
+        ],
+        compiler_params=pltpu.CompilerParams(
+            collective_id=slot, has_side_effects=True, vmem_limit_bytes=60 * 1024 * 1024
+        ),
+        name="reduce",
+    )(part)
 
 
 def whole(count):
@@ -637,13 +1076,12 @@
     )(patches, items, qkv_w, proj_w, gains, table)
 
 
-def run_experts(nm, upstream, ids, router_w, inner_w, down_w):
+def run_experts(nm, upstream, ids, router_w, weights, hidden):
     packs, length, width = nm.shape
-    experts = router_w.shape[0]
-    hidden = down_w.shape[1]
+    experts, copies, rows, _ = weights.shape
     cap = 2 * length * 2 // experts
     fixed3 = lambda e: (0, 0, 0)
-    each = lambda e: (e, 0, 0)
+    each = lambda e: (e, 0, 0, 0)
     grid_spec = pltpu.PrefetchScalarGridSpec(
         num_scalar_prefetch=0,
         grid=(experts,),
@@ -652,12 +1090,10 @@
             pl.BlockSpec((packs, length, width), fixed3),
             pl.BlockSpec((packs, 2, length), fixed3),
             pl.BlockSpec((experts, width), lambda e: (0, 0)),
-            pl.BlockSpec((1, width, 2 * hidden), each),
-            pl.BlockSpec((1, hidden, width), each),
+            pl.BlockSpec((1, copies, rows, width), each),
         ],
         out_specs=(
-            pl.BlockSpec((1, width, 2 * hidden), each),
-            pl.BlockSpec((1, hidden, width), each),
+            pl.BlockSpec((1, copies, rows, width), each),
             pl.BlockSpec((packs, length, 2 * width), fixed3),
             pl.BlockSpec((packs, experts, length), fixed3),
         ),
@@ -671,41 +1107,44 @@
             pltpu.VMEM((packs * cap, width), BF16),
             pltpu.VMEM((packs * cap, 2 * hidden), BF16),
             pltpu.VMEM((packs, experts * cap, 2 * width), BF16),
+            pltpu.VMEM((width, 2 * hidden), BF16),
+            pltpu.VMEM((hidden, width), BF16),
         ],
     )
     return pl.pallas_call(
         expert_kernel,
         out_shape=(
-            jax.ShapeDtypeStruct((experts, width, 2 * hidden), BF16),
-            jax.ShapeDtypeStruct((experts, hidden, width), BF16),
+            jax.ShapeDtypeStruct(weights.shape, BF16),
             jax.ShapeDtypeStruct((packs, length, 2 * width), F32),
             jax.ShapeDtypeStruct((packs, experts, length), BF16),
         ),
         grid_spec=grid_spec,
         compiler_params=LIMIT,
         name="experts",
-    )(nm, upstream, ids, router_w, inner_w, down_w)
-
-
-def run_return(patches, upstream, items, qkv_w, proj_w, gains, table, mixed, probs, att, mid, nm, back, glog):
+    )(nm, upstream, ids, router_w, weights)
+
+
+def run_return(
+    tail_shape, patches, upstream, items, qkv_w, proj_w, gains, table, mixed, probs, att, mid, nm, back, glog
+):
     packs, length, width = patches.shape
     shapes = (
         jax.ShapeDtypeStruct((packs, length, width), BF16),
         jax.ShapeDtypeStruct((packs, length, width), F32),
-        jax.ShapeDtypeStruct((width, 4 * width), F32),
-        jax.ShapeDtypeStruct((16, width), F32),
+        jax.ShapeDtypeStruct(tail_shape, BF16),
     )
     return pl.pallas_call(
         return_kernel,
         out_shape=shapes,
         in_specs=whole(14),
-        out_specs=tuple(whole(4)),
+        out_specs=tuple(whole(3)),
         scratch_shapes=[
             pltpu.VMEM((packs * length, width), BF16),
             pltpu.VMEM((packs * length, width), BF16),
             pltpu.VMEM((length, width), BF16),
             pltpu.VMEM((packs * length, 3 * width), BF16),
             pltpu.VMEM((length, 3 * width), F32),
+            pltpu.VMEM((16, width), F32),
         ],
         compiler_params=LIMIT,
         name="backward",
@@ -723,29 +1162,43 @@
 ):
     width = patches.shape[2]
     experts = router_master.shape[1]
-    inner_w = lax.all_gather(inner_master.astype(BF16), "dp", axis=1, tiled=True)
-    inner_w = lax.all_gather(inner_w, "expert", axis=0, tiled=True)
-    down_w = lax.all_gather(down_master.astype(BF16), "dp", axis=1, tiled=True)
-    down_w = lax.all_gather(down_w, "expert", axis=0, tiled=True)
+    hidden = down_master.shape[1] * lax.axis_size("dp")
+    devices = lax.axis_size("dp") * lax.axis_size("expert")
+    deep = inner_master.shape[1]
+    blocks = inner_master.shape[2] // width
+    shard = jnp.concatenate(
+        [
+            jnp.swapaxes(inner_master[0].reshape(deep, blocks, width), 0, 1).reshape(blocks * deep, width),
+            down_master[0],
+        ],
+        axis=0,
+    ).astype(BF16)
+    weights = run_gather(shard, 0)
     qkv_w = qkv_master.astype(BF16)
     proj_w = proj_master.astype(BF16)
     router_w = router_master.T.astype(BF16)
     ids = jnp.swapaxes(expert_ids, 1, 2)
     table = jnp.asarray(rope_table(QB))
+    tail_shape = (lax.axis_size("expert"), lax.axis_size("dp"), tail_rows(width, devices), width)
     mixed, probs, att, mid, nm = run_attend(patches, item_ids, qkv_w, proj_w, gains_master, table)
-    inner_g, down_g, back, glog = run_experts(nm, out_grad, ids, router_w, inner_w, down_w)
-    block_out, patch_grad, attn_g, small_g = run_return(
+    part, back, glog = run_experts(nm, out_grad, ids, router_w, weights, hidden)
+    block_out, patch_grad, tail = run_return(
+        tail_shape,
         patches, out_grad, item_ids, qkv_w, proj_w, gains_master, table, mixed, probs, att, mid, nm, back, glog
     )
-    grad_inner = lax.psum_scatter(inner_g, "expert", scatter_dimension=0, tiled=True)
-    grad_inner = lax.psum_scatter(grad_inner, "dp", scatter_dimension=1, tiled=True).astype(F32)
-    grad_down = lax.psum_scatter(down_g, "expert", scatter_dimension=0, tiled=True)
-    grad_down = lax.psum_scatter(grad_down, "dp", scatter_dimension=1, tiled=True).astype(F32)
-    attn_g, small_g = lax.psum((attn_g, small_g), ("dp", "expert"))
-    qkv_new = adamw(qkv_master, qkv_first, qkv_second, attn_g[:, : 3 * width], 0.1, 0.1)
-    proj_new = adamw(proj_master, proj_first, proj_second, attn_g[:, 3 * width :], 0.4, 0.1)
-    router_new = adamw(router_master, router_first, router_second, small_g[:experts].T, 0.07, 0.1)
-    gains_new = adamw(gains_master, gains_first, gains_second, small_g[experts : experts + 2], 0.4, 0.0)
+    grad = run_reduce(part, 1)
+    grad_inner = jnp.swapaxes(grad[: blocks * deep].reshape(blocks, deep, width), 0, 1).reshape(
+        inner_master.shape
+    )
+    grad_down = grad[blocks * deep :].reshape(down_master.shape)
+    tail = run_gather(run_reduce(tail, 2).astype(BF16), 3).astype(F32)
+    small = tail[0, 0, tail_shape[2] - 16 :]
+    attn = tail[:, :, : tail_shape[2] - 16].reshape(4, width, width)
+    grad_qkv = jnp.swapaxes(attn[:3], 0, 1).reshape(width, 3 * width)
+    qkv_new = adamw(qkv_master, qkv_first, qkv_second, grad_qkv, 0.1, 0.1)
+    proj_new = adamw(proj_master, proj_first, proj_second, attn[3], 0.4, 0.1)
+    router_new = adamw(router_master, router_first, router_second, small[:experts].T, 0.07, 0.1)
+    gains_new = adamw(gains_master, gains_first, gains_second, small[experts : experts + 2], 0.4, 0.0)
     inner_new = adamw(inner_master, inner_first, inner_second, grad_inner, 0.1, 0.1)
     down_new = adamw(down_master, down_first, down_second, grad_down, 0.15, 0.1)
     return (block_out, patch_grad) + qkv_new + proj_new + router_new + gains_new + inner_new + down_new
@@ -759,7 +1212,8 @@
     experts = inner_master.shape[0] * lax.axis_size("expert")
     entries = inner_master.shape[1] * inner_master.shape[2] + down_master.shape[1] * down_master.shape[2]
     weight_bytes = 2 * experts * entries * lax.axis_size("dp")
-    return (fast if weight_bytes <= GATHER_LIMIT else local)(*args)
+    square = lax.axis_size("dp") == 4 and inner_master.shape[0] == 1 and lax.axis_size("expert") == experts
+    return (fast if square and weight_bytes <= GATHER_LIMIT else local)(*args)
 
 
 def solution(mesh):

time: 780 us -> 354 us (0.45)
  waiting for transfers between devices: 570 us -> 0 us
  Pallas kernels: 125 us -> 308 us
  blocking collectives: 49.9 us -> 0 us
  local copies, waits for them, and re-layouts: 0.06 us -> 17.9 us
  between operations: 14.2 us -> 1.34 us
    reduce_scatter x4 -> x0, waiting for transfers between devices: 269 us -> none  [the longest x1 165 us: fast(): lax.psum_scatter(inner_g, 'expert', scatter_dimension=0, tiled=True)]
    all_gather x3 -> x0, waiting for transfers between devices: 203 us -> none  [the longest x1 138 us: fast(): inner_w = lax.all_gather(inner_w, 'expert', axis=0, tiled=True)]
    pallas_call x1 -> x5, Pallas kernels: 68.7 us -> 252 us  [the longest x2 90.5 us: run_gather(): pl.pallas_call(functools.partial(gather_kernel, line), out_shape=jax.Shap...]
    psum x1 -> x0, waiting for transfers between devices: 97.5 us -> none  [fast(): attn_g, small_g = lax.psum((attn_g, small_g), ('dp', 'expert'))]
    psum x1 -> x0, blocking collectives: 40.4 us -> none  [fast(): attn_g, small_g = lax.psum((attn_g, small_g), ('dp', 'expert'))]
    unnamed x28 -> x44, local copies, waits for them, and re-layouts: 0.06 us -> 12.8 us
    all_gather x1 -> x0, blocking collectives: 9.58 us -> none  [fast(): down_w = lax.all_gather(down_master.astype(BF16), 'dp', axis=1, tiled=True)]
  transfers between devices with their start and end apart: 8 -> 0, of which waited for: 8 -> 0; matrix products, arithmetic and copies ran while one was open for 2% -> 0% of each run, Pallas kernels for 7% -> 0%
where the time goes in v2:
time: 354 us; the launch traced here: 348 us
  Pallas kernels  308 us (87%)
  other arithmetic  20 us (6%)
  local copies, waits for them, and re-layouts  17.9 us (5%)
    pallas_call x2, Pallas kernels, run_gather(): pl.pallas_call(functools.partial(gather_kernel, line), out_shape=jax.Shap...  90.5 us
    pallas_call x2, Pallas kernels, run_reduce(): pl.pallas_call(functools.partial(reduce_kernel, line), out_shape=jax.Shap...  89.8 us
    pallas_call x1, Pallas kernels, run_experts(): pl.pallas_call(expert_kernel, out_shape=(jax.ShapeDtypeStruct(weights.sha...  72.1 us
    pallas_call x1, Pallas kernels, run_return(): pl.pallas_call(return_kernel, out_shape=shapes, in_specs=whole(14), out_s...  31.2 us
    pallas_call x1, Pallas kernels, run_attend(): pl.pallas_call(attend_kernel, out_shape=shapes, in_specs=whole(6), out_sp...  24.9 us
    sub x6, other arithmetic, adamw(): return (weight - rate * (update + decay * weight), first_new, second_new)  13.3 us
    unnamed x44, local copies, waits for them, and re-layouts  12.8 us

profile of v2, /device:TPU:0, one launch (start us, length us, event | category | flops | bytes accessed | tf_op | source)
XLA Modules:
  0.0 347.7 jit_solution(4389326931861621684)
XLA Ops:
  0.7 2.6 convert_element_type.18.qkv_w
  3.2 0.7 convert_element_type.19.proj_w
  4.0 24.9 %attend.1 = (bf16[3,512,1152]{2,1,0:T(8,128)(2,1)}, bf16[3,3,4,384,256]{4,3,2,1,0:T(8,128)(2,1)}, bf16[3,512,384]{2,1,0:T(8,128)(2,1)}, f32[3,512,384]{2,1,0:T(8,128)}, bf16[3,512,384]{2,1,0:T(8,128)(2,1)}) custom-call(bf16[3,512,384]{2,1,0:T(8,128)(2,1)} %patches.3, s32[3,1,512]{2,1,0:T(1,128)} %items.3, bf16[384,1152]{1,0:T(8,128)(2,1)} %convert_element_type.18.qkv_w, ...), custom_call_target="tpu_custom_call" | custom-call | tf_op jit(solution)/shard_map/attend/pallas_call | solution.py:1069
  29.6 0.8 pad_maximum_fusion.shard
  30.4 69.0 %gather.2.weights = bf16[8,4,576,384]{3,2,1,0:T(8,128)(2,1)} custom-call(bf16[576,384]{1,0:T(8,128)(2,1)} %pad_maximum_fusion.shard), custom_call_target="tpu_custom_call" | custom-call | tf_op jit(solution)/shard_map/gather/pallas_call | solution.py:840
  99.5 72.1 %experts.1 = (bf16[8,4,576,384]{3,2,1,0:T(8,128)(2,1)}, f32[3,512,768]{2,1,0:T(8,128)}, bf16[3,8,512]{2,1,0:T(8,128)(2,1)}) custom-call(bf16[3,512,384]{2,1,0:T(8,128)(2,1)} %get-tuple-element.35.nm, bf16[3,512,384]{2,1,0:T(8,128)(2,1)} %upstream.3, s32[3,2,512]{2,1,0:T(2,128)} %bitcast.55, bf16[8,384]{1,0:T(8,128)(2,1)} %convert_bitcast_fusion.1.router_w, ...), custom_call_target="tpu_custom_call" | custom-call | tf_op jit(solution)/shard_map/experts/pallas_call | solution.py:1114
  171.6 31.2 %backward.1 = (bf16[3,512,384]{2,1,0:T(8,128)(2,1)}, f32[3,512,384]{2,1,0:T(8,128)}, bf16[8,4,64,384]{3,2,1,0:T(8,128)(2,1)}) custom-call(bf16[3,512,384]{2,1,0:T(8,128)(2,1)} %patches.3, bf16[3,512,384]{2,1,0:T(8,128)(2,1)} %upstream.3, s32[3,1,512]{2,1,0:T(1,128)} %items.3, bf16[384,1152]{1,0:T(8,128)(2,1)} %convert_element_type.18.qkv_w, ...), custom_call_target="tpu_custom_call" | custom-call | tf_op jit(solution)/shard_map/backward/pallas_call | solution.py:1136
  202.8 1.2 copy.51
  204.0 21.7 %reduce.2 = f32[64,384]{1,0:T(8,128)} custom-call(bf16[8,4,64,384]{3,2,1,0:T(8,128)(2,1)} %get-tuple-element.40.part), custom_call_target="tpu_custom_call" | custom-call | tf_op jit(solution)/shard_map/reduce/pallas_call | solution.py:1035
  225.6 1.5 convert_element_type.22.shard
  227.2 21.5 %gather.3 = bf16[8,4,64,384]{3,2,1,0:T(8,128)(2,1)} custom-call(bf16[64,384]{1,0:T(8,128)(2,1)} %convert_element_type.22.shard), custom_call_target="tpu_custom_call" | custom-call | tf_op jit(solution)/shard_map/gather/pallas_call | solution.py:840
  248.7 1.3 slice.43
  250.0 1.8 copy.48
  251.8 2.9 copy.47
  254.7 1.7 copy.49
  256.4 5.6 %multiply_subtract_fusion = (f32[384,1152]{0,1:T(8,128)}, f32[384,1152]{0,1:T(8,128)}, f32[384,1152]{0,1:T(8,128)S(1)}) fusion(f32[384,1152]{0,1:T(8,128)S(1)} %copy.51, f32[3,384,384]{1,2,0:T(8,128)} %copy.48, f32[384,1152]{0,1:T(8,128)} %copy.47, f32[384,1152]{0,1:T(8,128)} %copy.49), kind=kLoop, calls=%fused_computation.3 | loop fusion | flops 6193152 | bytes 12386304 | tf_op jit(solution)/shard_map/sub | solution.py:56
  262.0 2.9 copy.53
  264.9 1.9 copy.54
  266.8 1.9 copy.55
  268.7 3.0 multiply_subtract_fusion.2
  273.6 68.1 %reduce.3 = f32[576,384]{1,0:T(8,128)} custom-call(bf16[8,4,576,384]{3,2,1,0:T(8,128)(2,1)} %get-tuple-element.41.part), custom_call_target="tpu_custom_call" | custom-call | tf_op jit(solution)/shard_map/reduce/pallas_call | solution.py:1035
  341.8 1.2 slice.41
  343.7 1.5 multiply_subtract_fusion.1
  345.2 2.0 multiply_subtract_fusion.3
  (49 shorter events, 3.4 us)
Async XLA Ops:
  0.7 2.6 copy-start.3
  3.2 25.6 %copy-start.13 = (f32[384,8]{0,1:T(8,128)S(1)}, f32[384,8]{0,1:T(8,128)}, u32[]{:S(2)}) copy-start(f32[384,8]{0,1:T(8,128)} %param.33) | copy-start | bytes 36868
  3.2 26.2 %copy-start.7 = (f32[1,192,384]{2,1,0:T(8,128)S(1)}, f32[1,192,384]{2,1,0:T(8,128)}, u32[]{:S(2)}) copy-start(f32[1,192,384]{2,1,0:T(8,128)} %param.42) | copy-start | bytes 884740
  3.2 26.2 %copy-start.4 = (f32[1,96,1536]{2,1,0:T(8,128)S(1)}, f32[1,96,1536]{2,1,0:T(8,128)}, u32[]{:S(2)}) copy-start(f32[1,96,1536]{2,1,0:T(8,128)} %param.39) | copy-start | bytes 1769476
  171.6 31.2 %copy-start.2 = (f32[384,1152]{1,0:T(8,128)S(1)}, f32[384,1152]{1,0:T(8,128)}, u32[]{:S(2)}) copy-start(f32[384,1152]{1,0:T(8,128)} %param.27) | copy-start | bytes 5308420
  251.8 2.9 copy-start.6
  262.0 2.9 copy-start.1
  266.8 1.9 copy-start
  271.7 0.7 copy-start.15
  271.7 0.7 copy-start.16
  271.7 1.3 copy-start.14
  271.7 1.3 copy-start.17
  271.7 1.3 copy-start.18
  341.7 1.9 copy-start.5
  341.8 1.9 copy-start.9
  341.8 1.9 copy-start.10
  343.7 1.5 copy-start.8
  343.7 1.5 copy-start.11
  343.7 1.5 copy-start.12
